TPU v7x, 32 devices: a whole 2x2x4 slice. The times are simulated.
32 devices in a mesh: seq: 16 (over z, y, core), head: 2 (over x).
Axes of the slice: x: 2, y: 2, z: 4, core: 2. Of those that a mesh axis runs over, the one named last changes fastest.
Arguments:
- q_nope: bfloat16 [4096, 8192], P('seq', 'head'), may hold values from -6 to 6
- q_rope: bfloat16 [4096, 4096], P('seq', 'head'), may hold values from -8 to 8
- latent: bfloat16 [4096, 576], P('seq'), may hold values from -8 to 8
- doc_ids: int32 [4096], P('seq'), may hold values from 0 to 15, never falling along the last dimension, each value on 1 to 1280 neighbouring positions
- w_uk: bfloat16 [512, 8192], P(None, 'head'), may hold values from -0.25 to 0.25
- w_uv: bfloat16 [512, 8192], P(None, 'head'), may hold values from -0.25 to 0.25
- w_out: bfloat16 [8192, 3584], P('head', 'seq'), may hold values from -0.375 to 0.375
Outputs:
- projected: bfloat16 [4096, 3584], P('seq', 'head')
Inputs may be any that keep to these rules, and one draw needn't show every extreme that they name: `doc_ids`: document ids never fall along the sequence; every document holds 1 to 1280 tokens, and one holds exactly that many.
All inputs are finite; a program needn't handle non-finite values.
Results may differ from a plain program's by a relative error of at most 0.0065.
Values may be sent and summed in bfloat16 or wider, within the bound.
A program may use at most 128 MiB of HBM per device.

v0:
```python
import math

import jax
import jax.numpy as jnp
from jax import lax
from jax.sharding import PartitionSpec as P

HD = 128
ROPE = 64
VD = 128
LAT = 512
HOPS = 4


def from_behind(value, axis, steps):
    count = lax.axis_size(axis)
    leading, last = (max(0, -steps), min(count, count - steps))
    return lax.ppermute(value, axis, [(source, source + steps) for source in range(leading, last)])


def shards(q_nope, q_rope, latent, doc_ids, w_uk, w_uv, w_out):
    tok_rows = q_nope.shape[0]
    head_count = w_uk.shape[1] // HD
    score_scale = 1.0 / math.sqrt(HD + ROPE)
    w_whole = lax.all_gather(w_out, "seq", axis=1, tiled=True)
    position = lax.axis_index("seq")
    doc_marks = doc_ids.astype(jnp.bfloat16)
    latent_list = [latent]
    doc_list = [doc_marks]
    moving = (latent, doc_marks)
    for distance in range(1, HOPS + 1):
        moving = from_behind((moving[0], moving[1]), "seq", 1)
        latent_list.append(moving[0])
        doc_list.append(moving[1])
    local_iota = jnp.arange(tok_rows, dtype=jnp.int32)
    key_pos = jnp.concatenate(
        [(position - distance) * tok_rows + local_iota for distance in range(HOPS + 1)]
    )
    key_latent = jnp.concatenate(latent_list, axis=0)
    key_doc = jnp.concatenate(doc_list, axis=0).astype(jnp.float32)
    query_pos = position * tok_rows + local_iota
    separation = query_pos[:, None] - key_pos[None, :]
    allowed = (key_pos[None, :] >= 0) & (separation >= 0) & (separation < HOPS * tok_rows)
    allowed = allowed & (doc_ids.astype(jnp.float32)[:, None] == key_doc[None, :])
    content = key_latent[:, :LAT]
    key_rope = key_latent[:, LAT:]
    key_weights = w_uk.reshape(LAT, head_count, HD).transpose(1, 0, 2)
    value_weights = w_uv.reshape(LAT, head_count, VD).transpose(1, 0, 2)
    query_nope = q_nope.reshape(tok_rows, head_count, HD).transpose(1, 0, 2)
    query_rope = q_rope.reshape(tok_rows, head_count, ROPE).transpose(1, 0, 2)

    def one_head(pieces):
        key_map, value_map, head_nope, head_rope = pieces
        key_nope = jnp.dot(content, key_map, preferred_element_type=jnp.float32).astype(
            jnp.bfloat16
        )
        values = jnp.dot(content, value_map, preferred_element_type=jnp.float32).astype(
            jnp.bfloat16
        )
        scores = jnp.dot(head_nope, key_nope.T, preferred_element_type=jnp.float32)
        scores = (
            scores + jnp.dot(head_rope, key_rope.T, preferred_element_type=jnp.float32)
        ) * score_scale
        scores = jnp.where(allowed, scores, jnp.float32(-1e30))
        row_max = jnp.max(scores, axis=-1, keepdims=True)
        raw_weights = jnp.where(allowed, jnp.exp(scores - row_max), jnp.float32(0.0))
        weights_half = (raw_weights / jnp.sum(raw_weights, axis=-1, keepdims=True)).astype(
            jnp.bfloat16
        )
        return jnp.dot(weights_half, values, preferred_element_type=jnp.float32).astype(
            jnp.bfloat16
        )

    per_head = lax.map(one_head, (key_weights, value_weights, query_nope, query_rope))
    attended = per_head.transpose(1, 0, 2).reshape(tok_rows, head_count * VD)
    partial_out = jnp.dot(attended, w_whole, preferred_element_type=jnp.float32)
    return lax.psum_scatter(partial_out, "head", scatter_dimension=1, tiled=True).astype(
        jnp.bfloat16
    )


def solution(mesh):
    placed = (
        P("seq", "head"),
        P("seq", "head"),
        P("seq", None),
        P("seq"),
        P(None, "head"),
        P(None, "head"),
        P("head", "seq"),
    )
    return jax.shard_map(
        shards, mesh=mesh, in_specs=placed, out_specs=P("seq", "head"), check_vma=False
    )
```

profile of v0, /device:TPU:4, one launch (start us, length us, event | category | flops | bytes accessed | tf_op | source)
XLA Modules:
  0.0 443.1 jit_solution(9546071359713848969)
XLA Ops:
  9.5 3.5 collective-permute-start
  13.1 5.2 %collective-permute-done = bf16[256,576]{1,0:T(8,128)(2,1)S(1)} collective-permute-done((bf16[256,576]{1,0:T(8,128)(2,1)S(1)}, bf16[256,576]{1,0:T(8,128)(2,1)S(1)}, u32[]{:S(2)}, u32[]{:S(2)}) %collective-permute-start) | collective-permute-done | bytes 294944 | tf_op jit(solution)/shard_map/ppermute | solution.py:18
  20.3 13.5 %collective-permute-done.1 = bf16[256,576]{1,0:T(8,128)(2,1)} collective-permute-done((bf16[256,576]{1,0:T(8,128)(2,1)S(1)}, bf16[256,576]{1,0:T(8,128)(2,1)}, u32[]{:S(2)}, u32[]{:S(2)}) %collective-permute-start.1) | collective-permute-done | bytes 294944 | tf_op jit(solution)/shard_map/ppermute | solution.py:18
  35.8 4.9 %collective-permute-start.5 = (bf16[256]{0:T(256)(128)(2,1)S(1)}, bf16[256]{0:T(256)(128)(2,1)S(1)}, u32[]{:S(2)}, u32[]{:S(2)}) collective-permute-start(bf16[256]{0:T(256)(128)(2,1)S(1)} %collective-permute-done.4), channel_id=1, source_target_pairs={{0,2},{2,4},{4,6},{6,8},{8,10},{10,12},{12,14},{14,16},{16,18},{18... | collective-permute-start | bytes 1544 | tf_op jit(solution)/shard_map/ppermute | solution.py:18
  40.7 8.8 %collective-permute-done.5 = bf16[256]{0:T(256)(128)(2,1)S(1)} collective-permute-done((bf16[256]{0:T(256)(128)(2,1)S(1)}, bf16[256]{0:T(256)(128)(2,1)S(1)}, u32[]{:S(2)}, u32[]{:S(2)}) %collective-permute-start.5) | collective-permute-done | bytes 544 | tf_op jit(solution)/shard_map/ppermute | solution.py:18
  49.5 2.4 collective-permute-start.6
  52.0 6.5 %copy.11 = bf16[512,4096]{0,1:T(8,128)(2,1)} copy(bf16[512,4096]{1,0:T(8,128)(2,1)} %param.13) | data formatting | bytes 8388608 | tf_op args[4]
  58.5 6.5 %copy.15 = bf16[512,4096]{0,1:T(8,128)(2,1)} copy(bf16[512,4096]{1,0:T(8,128)(2,1)} %param.14) | data formatting | bytes 8388608 | tf_op args[5]
  65.0 4.2 copy.10
  70.5 5.3 %collective-permute-start.7 = (bf16[256]{0:T(256)(128)(2,1)S(1)}, bf16[256]{0:T(256)(128)(2,1)S(1)}, u32[]{:S(2)}, u32[]{:S(2)}) collective-permute-start(bf16[256]{0:T(256)(128)(2,1)S(1)} %collective-permute-done.6), channel_id=1, source_target_pairs={{0,2},{2,4},{4,6},{6,8},{8,10},{10,12},{12,14},{14,16},{16,18},{18... | collective-permute-start | bytes 1544 | tf_op jit(solution)/shard_map/ppermute | solution.py:18
  76.7 2.1 collective-permute-start.3
  80.9 11.4 %collective-permute-done.3 = bf16[256,576]{1,0:T(8,128)(2,1)S(1)} collective-permute-done((bf16[256,576]{1,0:T(8,128)(2,1)}, bf16[256,576]{1,0:T(8,128)(2,1)S(1)}, u32[]{:S(2)}, u32[]{:S(2)}) %collective-permute-start.3) | collective-permute-done | bytes 294944 | tf_op jit(solution)/shard_map/ppermute | solution.py:18
  92.4 274.0 %while.11 = (s32[]{:T(128)}, bf16[32,256,128]{1,2,0:T(8,128)(2,1)}, bf16[32,256,128]{1,2,0:T(8,128)(2,1)}, bf16[32,512,128]{1,2,0:T(8,128)(2,1)}, bf16[1280,512]...) while((s32[]{:T(128)}, bf16[32,256,128]{1,2,0:T(8,128)(2,1)}, ...), condition=%wide.region_3.4_spmd.clone, body=%wide.region_0.3_spmd.clone.sunk | while | flops 556105216 | bytes 15318433 | solution.py:74
  97.8 2.6 fusion.61
  106.5 2.5 fusion.61
  115.0 2.5 fusion.61
  123.6 2.5 fusion.61
  132.2 2.6 fusion.61
  140.9 2.5 fusion.61
  149.5 2.5 fusion.61
  158.0 2.5 fusion.61
  166.5 2.6 fusion.61
  175.2 2.5 fusion.61
  183.7 2.5 fusion.61
  192.3 2.5 fusion.61
  200.8 2.5 fusion.61
  209.4 2.5 fusion.61
  217.9 2.5 fusion.61
  226.5 2.5 fusion.61
  235.0 2.5 fusion.61
  243.6 2.5 fusion.61
  252.1 2.5 fusion.61
  260.7 2.5 fusion.61
  269.2 2.5 fusion.61
  277.8 2.5 fusion.61
  286.3 2.5 fusion.61
  294.9 2.5 fusion.61
  303.4 2.5 fusion.61
  311.9 2.5 fusion.61
  320.5 2.5 fusion.61
  329.0 2.5 fusion.61
  337.6 2.5 fusion.61
  346.1 2.5 fusion.61
  354.6 2.5 fusion.61
  363.2 2.5 fusion.61
  366.4 15.3 %fusion.36 = f32[256,3584]{1,0:T(8,128)} fusion(bf16[256,4096]{0,1:T(8,128)(2,1)} %bitcast.62, bf16[4096,3584]{0,1:T(8,128)(2,1)} %all-gather.2.cloned.1.call-done), kind=kOutput, calls=%fused_computation.49 | convolution fusion | flops 7516192768 | bytes 35127296 | tf_op jit(solution)/shard_map/dot_general | solution.py:76
  381.8 52.0 %reduce-scatter.2.cloned.1.call-done = f32[256,1792]{1,0:T(8,128)} async-done(((f32[256,3584]{1,0:T(8,128)}), f32[256,1792]{1,0:T(8,128)}) %reduce-scatter.2.cloned.1.call-update) | async-done | bytes 1835024 | tf_op jit(solution)/shard_map/reduce_scatter | solution.py:77
  433.8 2.5 convert_element_type.33
  (268 shorter events, 205.2 us)
Async XLA Ops:
  6.5 0.8 copy-start.3
  6.5 2.7 copy-start.2
  6.5 359.9 %all-gather.2.cloned.1.call-start = ((), (), s32[]{:S(2)}) async-start(), calls=%async_computation.1 | async-start | bytes 31195136 | tf_op jit(solution)/shard_map/all_gather | solution.py:25
  7.3 426.5 %reduce-scatter.2.cloned.1.call-start = ((), (), s32[]{:S(2)}) async-start(), calls=%async_computation.2 | async-start | bytes 5505024 | tf_op jit(solution)/shard_map/reduce_scatter | solution.py:77
  7.3 28.4 %collective-permute-start.4 = (bf16[256]{0:T(256)(128)(2,1)S(1)}, bf16[256]{0:T(256)(128)(2,1)S(1)}, u32[]{:S(2)}, u32[]{:S(2)}) collective-permute-start(bf16[256]{0:T(256)(128)(2,1)S(1)} %get-tuple-element.128), channel_id=1, source_target_pairs={{0,2},{2,4},{4,6},{6,8},{8,10},{10,12},{12,14},{14,16},{16,18},{18... | collective-permute-start | bytes 1544 | tf_op jit(solution)/shard_map/ppermute | solution.py:18
  9.5 8.9 %collective-permute-start = (bf16[256,576]{1,0:T(8,128)(2,1)S(1)}, bf16[256,576]{1,0:T(8,128)(2,1)S(1)}, u32[]{:S(2)}, u32[]{:S(2)}) collective-permute-start(bf16[256,576]{1,0:T(8,128)(2,1)S(1)} %copy.13), channel_id=1, source_target_pairs={{0,2},{2,4},{4,6},{6,8},{8,10},{10,12},{12,14},{14,16},{16,18},{18... | collective-permute-start | bytes 884744 | tf_op jit(solution)/shard_map/ppermute | solution.py:18
  18.3 15.5 %collective-permute-start.1 = (bf16[256,576]{1,0:T(8,128)(2,1)S(1)}, bf16[256,576]{1,0:T(8,128)(2,1)}, u32[]{:S(2)}, u32[]{:S(2)}) collective-permute-start(bf16[256,576]{1,0:T(8,128)(2,1)S(1)} %collective-permute-done), channel_id=1, source_target_pairs={{0,2},{2,4},{4,6},{6,8},{8,10},{10,12},{12,14},{14,16},{16,18},{18... | collective-permute-start | bytes 884744 | tf_op jit(solution)/shard_map/ppermute | solution.py:18
  33.8 42.8 %collective-permute-start.2 = (bf16[256,576]{1,0:T(8,128)(2,1)}, bf16[256,576]{1,0:T(8,128)(2,1)}, u32[]{:S(2)}, u32[]{:S(2)}) collective-permute-start(bf16[256,576]{1,0:T(8,128)(2,1)} %collective-permute-done.1), channel_id=1, source_target_pairs={{0,2},{2,4},{4,6},{6,8},{8,10},{10,12},{12,14},{14,16},{16,18},{18... | collective-permute-start | bytes 884744 | tf_op jit(solution)/shard_map/ppermute | solution.py:18
  35.8 13.7 %collective-permute-start.5 = (bf16[256]{0:T(256)(128)(2,1)S(1)}, bf16[256]{0:T(256)(128)(2,1)S(1)}, u32[]{:S(2)}, u32[]{:S(2)}) collective-permute-start(bf16[256]{0:T(256)(128)(2,1)S(1)} %collective-permute-done.4), channel_id=1, source_target_pairs={{0,2},{2,4},{4,6},{6,8},{8,10},{10,12},{12,14},{14,16},{16,18},{18... | collective-permute-start | bytes 1544 | tf_op jit(solution)/shard_map/ppermute | solution.py:18
  49.5 21.0 %collective-permute-start.6 = (bf16[256]{0:T(256)(128)(2,1)S(1)}, bf16[256]{0:T(256)(128)(2,1)S(1)}, u32[]{:S(2)}, u32[]{:S(2)}) collective-permute-start(bf16[256]{0:T(256)(128)(2,1)S(1)} %collective-permute-done.5), channel_id=1, source_target_pairs={{0,2},{2,4},{4,6},{6,8},{8,10},{10,12},{12,14},{14,16},{16,18},{18... | collective-permute-start | bytes 1544 | tf_op jit(solution)/shard_map/ppermute | solution.py:18
  65.0 4.2 copy-start.1
  70.5 6.2 %collective-permute-start.7 = (bf16[256]{0:T(256)(128)(2,1)S(1)}, bf16[256]{0:T(256)(128)(2,1)S(1)}, u32[]{:S(2)}, u32[]{:S(2)}) collective-permute-start(bf16[256]{0:T(256)(128)(2,1)S(1)} %collective-permute-done.6), channel_id=1, source_target_pairs={{0,2},{2,4},{4,6},{6,8},{8,10},{10,12},{12,14},{14,16},{16,18},{18... | collective-permute-start | bytes 1544 | tf_op jit(solution)/shard_map/ppermute | solution.py:18
  76.7 15.6 %collective-permute-start.3 = (bf16[256,576]{1,0:T(8,128)(2,1)}, bf16[256,576]{1,0:T(8,128)(2,1)S(1)}, u32[]{:S(2)}, u32[]{:S(2)}) collective-permute-start(bf16[256,576]{1,0:T(8,128)(2,1)} %collective-permute-done.2), channel_id=1, source_target_pairs={{0,2},{2,4},{4,6},{6,8},{8,10},{10,12},{12,14},{14,16},{16,18},{18... | collective-permute-start | bytes 884744 | tf_op jit(solution)/shard_map/ppermute | solution.py:18
  95.9 1.1 copy-start
  104.6 1.1 copy-start
  113.1 1.1 copy-start
  121.7 1.1 copy-start
  130.3 1.1 copy-start
  139.0 1.1 copy-start
  147.6 1.1 copy-start
  156.1 1.1 copy-start
  164.6 1.1 copy-start
  173.3 1.1 copy-start
  181.8 1.1 copy-start
  190.4 1.1 copy-start
  198.9 1.1 copy-start
  207.5 1.1 copy-start
  216.0 1.1 copy-start
  224.6 1.1 copy-start
  233.1 1.1 copy-start
  241.7 1.1 copy-start
  250.2 1.1 copy-start
  258.8 1.1 copy-start
  267.3 1.1 copy-start
  275.9 1.1 copy-start
  284.4 1.1 copy-start
  292.9 1.1 copy-start
  301.5 1.1 copy-start
  310.0 1.1 copy-start
  318.6 1.1 copy-start
  327.1 1.1 copy-start
  335.7 1.1 copy-start
  344.2 1.1 copy-start
  352.7 1.1 copy-start
  361.3 1.1 copy-start
Sparse Core Ops, SparseCore 0:
  9.0 159.2 all-gather.1
  381.9 51.8 reduce-scatter.1
where the time goes:
time: 449 us; the launch traced here: 443 us
  matrix products  204 us (45%)
  waiting for transfers between devices  91.7 us (20%)
  local copies, waits for them, and re-layouts  80.2 us (18%)
  other arithmetic  29 us (6%)
  starting transfers between devices  24.1 us (5%)
  between operations  13.6 us (3%)
    dot_general x32, matrix products, one_head(): jnp.dot(weights_half, values, preferred_element_type=jnp.float32)  79.4 us
    dot_general x32, matrix products, one_head(): scores = jnp.dot(head_nope, key_nope.T, preferred_element_type=jnp.float32)  55.8 us
    dot_general x32, matrix products, one_head(): jnp.dot(head_rope, key_rope.T, preferred_element_type=jnp.float32)  53.4 us
    reduce_scatter x1, waiting for transfers between devices, shards(): lax.psum_scatter(partial_out, 'head', scatter_dimension=1, tiled=True)  52 us
    ppermute x8, waiting for transfers between devices, from_behind(): lax.ppermute(value, axis, [(source, source + steps) for source in range(l...  39 us
    while x64, local copies, waits for them, and re-layouts  34.3 us
    reduce_sum x32, other arithmetic, one_head(): jnp.sum(raw_weights, axis=-1, keepdims=True)  26.4 us
    dynamic_update_slice x64, local copies, waits for them, and re-layouts, shards(): lax.map(one_head, (key_weights, value_weights, query_nope, query_rope))  24.1 us
  transfers between devices with their start and end apart: 10, of which 5 were waited for; matrix products, arithmetic and copies ran while one was open for 59% of the time, Pallas kernels for 0%

commit v1 on v0

v1 whole, which is shorter than its diff:
```python
import functools
import math

import jax
import jax.numpy as jnp
from jax import lax
from jax.experimental import pallas as pl
from jax.experimental.pallas import tpu as pltpu
from jax.sharding import PartitionSpec as P

HD = 128
ROPE = 64
VD = 128
LAT = 512
HOPS = 4
MARKS = 64
FAR = 1e30
PIECES = 2


def from_behind(value, steps):
    count = lax.axis_size("seq")
    return lax.ppermute(value, "seq", [(source, source + steps) for source in range(count - steps)])


def attend(rows, q_nope, q_rope, q_mark, content, tails, w_uk, w_uv, out):
    scale = math.log2(math.e) / math.sqrt(HD + ROPE)
    keys = content.shape[0]
    key_pair = jnp.dot(content[...], w_uk[...], preferred_element_type=jnp.float32).astype(jnp.bfloat16)
    value_pair = jnp.dot(content[...], w_uv[...], preferred_element_type=jnp.float32).astype(jnp.bfloat16)
    causal = lax.broadcasted_iota(jnp.int32, (rows, rows), 1) <= lax.broadcasted_iota(jnp.int32, (rows, rows), 0)
    low = lax.broadcasted_iota(jnp.int32, (rows, 2 * ROPE), 1) < ROPE
    ones = jnp.ones((keys, VD), jnp.bfloat16)
    for half in range(2):
        cols = slice(half * HD, (half + 1) * HD)
        rope = jnp.where(low == (half == 0), q_rope[...], q_mark[...])
        query = jnp.concatenate([q_nope[:, cols], rope], axis=1)
        key = jnp.concatenate([key_pair[:, cols], tails[half]], axis=1)
        scores = lax.dot_general(query, key, (((1,), (1,)), ((), ())), preferred_element_type=jnp.float32)
        edge = jnp.where(causal, scores[:, keys - rows :], scores[:, :rows])
        joined = jnp.concatenate([edge, scores[:, rows : keys - rows]], axis=1)
        top = jnp.max(joined, axis=-1, keepdims=True)
        raw = jnp.exp2((joined - top) * scale).astype(jnp.bfloat16)
        near = jnp.where(causal, raw[:, :rows], jnp.bfloat16(0))
        far = jnp.where(causal, jnp.bfloat16(0), raw[:, :rows])
        weights = jnp.concatenate([far, raw[:, rows:], near], axis=1)
        value = jnp.concatenate([value_pair[:, cols], ones], axis=1)
        total = jnp.dot(weights, value, preferred_element_type=jnp.float32)
        out[:, cols] = (total[:, :VD] / total[:, VD:]).astype(jnp.bfloat16)


def attention(q_nope, q_rope, q_mark, content, tails, w_uk, w_uv):
    rows, width = q_nope.shape
    keys = content.shape[0]
    pairs = width // (2 * HD)
    whole = lambda *shape: pl.BlockSpec(shape, lambda i: (0,) * len(shape))
    return pl.pallas_call(
        functools.partial(attend, rows),
        out_shape=jax.ShapeDtypeStruct((rows, width), jnp.bfloat16),
        grid=(pairs,),
        in_specs=[
            pl.BlockSpec((rows, 2 * HD), lambda i: (0, i)),
            pl.BlockSpec((rows, 2 * ROPE), lambda i: (0, i)),
            whole(rows, 2 * ROPE),
            whole(keys, LAT),
            whole(2, keys, 2 * ROPE),
            pl.BlockSpec((LAT, 2 * HD), lambda i: (0, i)),
            pl.BlockSpec((LAT, 2 * HD), lambda i: (0, i)),
        ],
        out_specs=pl.BlockSpec((rows, 2 * VD), lambda i: (0, i)),
        compiler_params=pltpu.CompilerParams(
            dimension_semantics=("arbitrary",), vmem_limit_bytes=48 << 20
        ),
        cost_estimate=pl.CostEstimate(
            flops=pairs * 2 * keys * (2 * LAT * 2 * HD + 4 * rows * 2 * HD),
            bytes_accessed=2 * (rows * width * 3 + LAT * width * 2),
            transcendentals=pairs * 2 * rows * keys,
        ),
        name="attention",
    )(q_nope, q_rope, q_mark, content, tails, w_uk, w_uv)


def shards(q_nope, q_rope, latent, doc_ids, w_uk, w_uv, w_out):
    rows = q_nope.shape[0]
    count = lax.axis_size("seq")
    position = lax.axis_index("seq")
    w_rows = w_out.T
    step = w_rows.shape[0] // PIECES
    gathered = [
        lax.all_gather(w_rows[i * step : (i + 1) * step], "seq", axis=0, tiled=True)
        for i in range(PIECES)
    ]
    marks = (doc_ids[:, None] == jnp.arange(MARKS, dtype=jnp.int32)[None, :]).astype(jnp.bfloat16)
    payload = jnp.concatenate([latent, marks], axis=1)
    blocks = []
    for distance in range(HOPS, 0, -1):
        block = from_behind(payload, distance)
        blocks.append(
            jnp.concatenate(
                [block[:, : LAT + ROPE], jnp.where(position >= distance, block[:, LAT + ROPE :], jnp.bfloat16(1))],
                axis=1,
            )
        )
    blocks.append(payload)
    behind = jnp.concatenate(blocks, axis=0)
    content = behind[:, :LAT]
    key_rope, key_marks = behind[:, LAT : LAT + ROPE], behind[:, LAT + ROPE :]
    tails = jnp.stack(
        [jnp.concatenate([key_rope, key_marks], axis=1), jnp.concatenate([key_marks, key_rope], axis=1)]
    )
    q_mark = (marks - jnp.bfloat16(1)) * jnp.bfloat16(FAR)
    q_mark = jnp.concatenate([q_mark, q_mark], axis=1)
    attended = attention(q_nope, q_rope, q_mark, content, tails, w_uk, w_uv)
    heads = lax.axis_size("head")
    mine = lax.axis_index("head")
    swap = [(a, b) for a in range(heads) for b in range(heads) if a != b]
    parts = []
    for piece in gathered:
        share = lax.dot_general(
            attended, piece, (((1,), (1,)), ((), ())), preferred_element_type=jnp.float32
        )
        parts.append(lax.psum_scatter(share, "head", scatter_dimension=1, tiled=True) if heads > 2 else exchange(share, mine))
    joined = jnp.stack([part.reshape(rows, count // heads, step) for part in parts], axis=2)
    return joined.reshape(rows, -1).astype(jnp.bfloat16)


def exchange(share, mine):
    half = share.shape[1] // 2
    first, second = share[:, :half], share[:, half:]
    keep = jnp.where(mine == 0, first, second)
    give = jnp.where(mine == 0, second, first).astype(jnp.bfloat16)
    return keep + lax.ppermute(give, "head", [(0, 1), (1, 0)]).astype(jnp.float32)


def solution(mesh):
    placed = (
        P("seq", "head"),
        P("seq", "head"),
        P("seq", None),
        P("seq"),
        P(None, "head"),
        P(None, "head"),
        P("head", "seq"),
    )
    return jax.shard_map(
        shards, mesh=mesh, in_specs=placed, out_specs=P("seq", "head"), check_vma=False
    )
```

time: 449 us -> 290 us (0.65)
  matrix products: 204 us -> 15.8 us
  waiting for transfers between devices: 91.7 us -> 194 us
  local copies, waits for them, and re-layouts: 80.2 us -> 8.72 us
  Pallas kernels: 0 us -> 34.9 us
  other arithmetic: 29 us -> 4.14 us
  starting transfers between devices: 24.1 us -> 15.3 us
    dot_general x97 -> x2, matrix products: 204 us -> 15.8 us  [shards(): lax.dot_general(attended, piece, (((1,), (1,)), ((), ())), preferred_elem...]
    all_gather x1 -> x2, waiting for transfers between devices: 0.01 us -> 155 us  [shards(): lax.all_gather(w_rows[i * step:(i + 1) * step], 'seq', axis=0, tiled=True)]
    reduce_scatter x1 -> x0, waiting for transfers between devices: 52 us -> none  [shards(): lax.psum_scatter(partial_out, 'head', scatter_dimension=1, tiled=True)]
    pallas_call x0 -> x1, Pallas kernels: none -> 34.9 us  [attention(): pl.pallas_call(functools.partial(attend, rows), out_shape=jax.ShapeDtypeS...]
    while x64 -> x0, local copies, waits for them, and re-layouts: 34.3 us -> none
    reduce_sum x32 -> x0, other arithmetic: 26.4 us -> none  [one_head(): jnp.sum(raw_weights, axis=-1, keepdims=True)]
    dynamic_update_slice x64 -> x0, local copies, waits for them, and re-layouts: 24.1 us -> none  [shards(): lax.map(one_head, (key_weights, value_weights, query_nope, query_rope))]
    unnamed x19 -> x15, local copies, waits for them, and re-layouts: 21.7 us -> 3.64 us
  transfers between devices with their start and end apart: 10 -> 8, of which waited for: 5 -> 6; matrix products, arithmetic and copies ran while one was open for 59% -> 7% of each run, Pallas kernels for 0% -> 12%
where the time goes in v1:
time: 290 us; the launch traced here: 287 us
  waiting for transfers between devices  194 us (67%)
  Pallas kernels  34.9 us (12%)
  matrix products  15.8 us (5%)
  starting transfers between devices  15.3 us (5%)
  between operations  13.6 us (5%)
  local copies, waits for them, and re-layouts  8.72 us (3%)
  other arithmetic  4.14 us (1%)
    all_gather x2, waiting for transfers between devices, shards(): lax.all_gather(w_rows[i * step:(i + 1) * step], 'seq', axis=0, tiled=True)  155 us
    pallas_call x1, Pallas kernels, attention(): pl.pallas_call(functools.partial(attend, rows), out_shape=jax.ShapeDtypeS...  34.9 us
    ppermute x4, waiting for transfers between devices, from_behind(): lax.ppermute(value, 'seq', [(source, source + steps) for source in range(...  28.8 us
    dot_general x2, matrix products, shards(): lax.dot_general(attended, piece, (((1,), (1,)), ((), ())), preferred_elem...  15.8 us
    ppermute x4, starting transfers between devices, from_behind(): lax.ppermute(value, 'seq', [(source, source + steps) for source in range(...  12.1 us
    ppermute x2, waiting for transfers between devices, exchange(): lax.ppermute(give, 'head', [(0, 1), (1, 0)]).astype(jnp.float32)  9.92 us
  transfers between devices with their start and end apart: 8, of which 6 were waited for; matrix products, arithmetic and copies ran while one was open for 7% of the time, Pallas kernels for 12%

profile of v1, /device:TPU:4, one launch (start us, length us, event | category | flops | bytes accessed | tf_op | source)
XLA Modules:
  0.0 286.8 jit_solution(752755257683265469)
XLA Ops:
  6.5 3.0 %fusion.1 = (bf16[112,4096]{1,0:T(8,128)(2,1)}, bf16[112,4096]{1,0:T(8,128)(2,1)}) fusion(bf16[224,4096]{1,0:T(8,128)(2,1)} %bitcast.19), kind=kLoop, calls=%fused_computation.22 | loop fusion | bytes 3670016 | tf_op jit(solution)/shard_map/slice | solution.py:90
  9.6 0.7 all-gather.5.cloned.1.call-update
  10.3 0.2 copy-done.5
  10.5 0.2 copy.10
  10.7 0.1 fusion
  10.8 0.1 pad_maximum_fusion.2
  10.9 3.5 %collective-permute-start = (bf16[256,640]{1,0:T(8,128)(2,1)S(1)}, bf16[256,640]{1,0:T(8,128)(2,1)S(1)}, u32[]{:S(2)}, u32[]{:S(2)}) collective-permute-start(bf16[256,640]{1,0:T(8,128)(2,1)S(1)} %pad_maximum_fusion.2), channel_id=1, source_target_pairs={{0,8},{2,10},{4,12},{6,14},{8,16},{10,18},{12,20},{14,22},{16,24},... | collective-permute-start | bytes 983048 | tf_op jit(solution)/shard_map/ppermute | solution.py:23
  14.4 2.6 collective-permute-start.1
  17.0 3.4 %collective-permute-start.2 = (bf16[256,640]{1,0:T(8,128)(2,1)S(1)}, bf16[256,640]{1,0:T(8,128)(2,1)S(1)}, u32[]{:S(2)}, u32[]{:S(2)}) collective-permute-start(bf16[256,640]{1,0:T(8,128)(2,1)S(1)} %pad_maximum_fusion.2), channel_id=1, source_target_pairs={{0,4},{2,6},{4,8},{6,10},{8,12},{10,14},{12,16},{14,18},{16,20},{1... | collective-permute-start | bytes 983048 | tf_op jit(solution)/shard_map/ppermute | solution.py:23
  20.4 2.6 collective-permute-start.3
  23.1 0.1 add_multiply_fusion
  23.2 0.1 pad_maximum_fusion.3.q_mark
  23.3 1.1 collective-permute-done
  24.4 0.1 slice_select_fusion.3
  24.5 0.1 maximum_dynamic-update-slice_fusion.3
  24.6 13.9 %collective-permute-done.1 = bf16[256,640]{1,0:T(8,128)(2,1)S(1)} collective-permute-done((bf16[256,640]{1,0:T(8,128)(2,1)S(1)}, bf16[256,640]{1,0:T(8,128)(2,1)S(1)}, u32[]{:S(2)}, u32[]{:S(2)}) %collective-permute-start.1) | collective-permute-done | bytes 327712 | tf_op jit(solution)/shard_map/ppermute | solution.py:23
  38.4 0.1 slice_select_fusion.2
  38.5 0.1 maximum_dynamic-update-slice_fusion.2
  38.6 13.8 %collective-permute-done.2 = bf16[256,640]{1,0:T(8,128)(2,1)S(1)} collective-permute-done((bf16[256,640]{1,0:T(8,128)(2,1)S(1)}, bf16[256,640]{1,0:T(8,128)(2,1)S(1)}, u32[]{:S(2)}, u32[]{:S(2)}) %collective-permute-start.2) | collective-permute-done | bytes 327712 | tf_op jit(solution)/shard_map/ppermute | solution.py:23
  52.5 0.1 slice_select_fusion.1
  52.6 0.1 maximum_dynamic-update-slice_fusion.1
  52.7 0.1 slice_select_fusion
  52.8 0.1 maximum_dynamic-update-slice_fusion
  52.9 0.1 constant_dynamic-update-slice_fusion
  53.0 0.1 slice.77.content
  53.1 0.2 fusion.2
  53.3 0.2 slice_bitcast_fusion
  53.5 0.1 pad_maximum_fusion.1.tails
  53.6 0.7 copy-done
  54.3 34.9 %attention.1 = bf16[256,4096]{1,0:T(8,128)(2,1)S(1)} custom-call(bf16[256,4096]{1,0:T(8,128)(2,1)} %q_nope.1, bf16[256,2048]{1,0:T(8,128)(2,1)S(1)} %copy-done, bf16[256,128]{1,0:T(8,128)(2,1)S(1)} %pad_maximum_fusion.3.q_mark, bf16[1280,512]{1,0:T(8,128)(2,1)S(1)} %slice.77.content, bf16[2,1280,128]{2,1,0:T(8,128)(2,1)S(1)} %pad_maximum_fusion.1.tails, ...), custom_call_target="tpu_custom_call" | custom-call | flops 21474836480 | bytes 14680064 | tf_op jit(solution)/shard_map/attention/pallas_call | solution.py:57
  89.2 51.3 %all-gather.3.cloned.1.call-done = bf16[1792,4096]{1,0:T(8,128)(2,1)} async-done(((bf16[112,4096]{1,0:T(8,128)(2,1)}), bf16[1792,4096]{1,0:T(8,128)(2,1)}) %all-gather.3.cloned.1.call-update) | async-done | bytes 14680080 | tf_op jit(solution)/shard_map/all_gather | solution.py:90
  140.5 7.8 %fusion.3 = f32[256,1792]{1,0:T(8,128)S(1)} fusion(bf16[256,4096]{1,0:T(8,128)(2,1)S(1)} %attention.1, bf16[1792,4096]{1,0:T(8,128)(2,1)} %all-gather.3.cloned.1.call-done), kind=kOutput, calls=%fused_computation.24 | convolution fusion | flops 3758096384 | bytes 18612224 | tf_op jit(solution)/shard_map/dot_general | solution.py:119
  148.4 1.2 copy-done.1
  149.6 0.1 select_convert_fusion.1
  149.7 1.5 collective-permute-start.4
  151.2 103.6 %all-gather.5.cloned.1.call-done = bf16[1792,4096]{1,0:T(8,128)(2,1)} async-done(((bf16[112,4096]{1,0:T(8,128)(2,1)}), bf16[1792,4096]{1,0:T(8,128)(2,1)}) %all-gather.5.cloned.1.call-update) | async-done | bytes 14680080 | tf_op jit(solution)/shard_map/all_gather | solution.py:90
  254.9 8.0 %fusion.4 = f32[256,1792]{1,0:T(8,128)S(1)} fusion(bf16[256,4096]{1,0:T(8,128)(2,1)S(1)} %attention.1, bf16[1792,4096]{1,0:T(8,128)(2,1)} %all-gather.5.cloned.1.call-done), kind=kOutput, calls=%fused_computation.25 | convolution fusion | flops 3758096384 | bytes 18612224 | tf_op jit(solution)/shard_map/dot_general | solution.py:119
  262.9 1.3 copy-done.3
  264.1 0.1 select_convert_fusion
  264.2 1.5 collective-permute-start.5
  265.7 1.2 add_convert_fusion.1
  266.9 0.2 copy.11
  267.1 9.9 %collective-permute-done.5 = bf16[256,896]{1,0:T(8,128)(2,1)} collective-permute-done((bf16[256,896]{1,0:T(8,128)(2,1)S(1)}, bf16[256,896]{1,0:T(8,128)(2,1)}, u32[]{:S(2)}, u32[]{:S(2)}) %collective-permute-start.5) | collective-permute-done | bytes 458784 | tf_op jit(solution)/shard_map/ppermute | solution.py:132
  277.1 1.1 add_convert_fusion
  278.2 0.2 copy.12
  278.4 0.1 pad_maximum_fusion
  278.5 0.1 copy.13
  278.6 1.4 copy.14
  (15 shorter events, 0.1 us)
Async XLA Ops:
  6.5 134.0 %all-gather.3.cloned.1.call-start = ((), (), s32[]{:S(2)}) async-start(), calls=%async_computation | async-start | bytes 15597568 | tf_op jit(solution)/shard_map/all_gather | solution.py:90
  9.5 1.0 copy-start.5
  9.5 1.2 copy-start.6
  9.5 245.3 %all-gather.5.cloned.1.call-start = ((), (), s32[]{:S(2)}) async-start(), calls=%async_computation.1 | async-start | bytes 15597568 | tf_op jit(solution)/shard_map/all_gather | solution.py:90
  10.9 13.5 %collective-permute-start = (bf16[256,640]{1,0:T(8,128)(2,1)S(1)}, bf16[256,640]{1,0:T(8,128)(2,1)S(1)}, u32[]{:S(2)}, u32[]{:S(2)}) collective-permute-start(bf16[256,640]{1,0:T(8,128)(2,1)S(1)} %pad_maximum_fusion.2), channel_id=1, source_target_pairs={{0,8},{2,10},{4,12},{6,14},{8,16},{10,18},{12,20},{14,22},{16,24},... | collective-permute-start | bytes 983048 | tf_op jit(solution)/shard_map/ppermute | solution.py:23
  14.4 24.0 %collective-permute-start.1 = (bf16[256,640]{1,0:T(8,128)(2,1)S(1)}, bf16[256,640]{1,0:T(8,128)(2,1)S(1)}, u32[]{:S(2)}, u32[]{:S(2)}) collective-permute-start(bf16[256,640]{1,0:T(8,128)(2,1)S(1)} %pad_maximum_fusion.2), channel_id=1, source_target_pairs={{0,6},{2,8},{4,10},{6,12},{8,14},{10,16},{12,18},{14,20},{16,22},{... | collective-permute-start | bytes 983048 | tf_op jit(solution)/shard_map/ppermute | solution.py:23
  17.0 35.5 %collective-permute-start.2 = (bf16[256,640]{1,0:T(8,128)(2,1)S(1)}, bf16[256,640]{1,0:T(8,128)(2,1)S(1)}, u32[]{:S(2)}, u32[]{:S(2)}) collective-permute-start(bf16[256,640]{1,0:T(8,128)(2,1)S(1)} %pad_maximum_fusion.2), channel_id=1, source_target_pairs={{0,4},{2,6},{4,8},{6,10},{8,12},{10,14},{12,16},{14,18},{16,20},{1... | collective-permute-start | bytes 983048 | tf_op jit(solution)/shard_map/ppermute | solution.py:23
  20.4 32.3 %collective-permute-start.3 = (bf16[256,640]{1,0:T(8,128)(2,1)S(1)}, bf16[256,640]{1,0:T(8,128)(2,1)S(1)}, u32[]{:S(2)}, u32[]{:S(2)}) collective-permute-start(bf16[256,640]{1,0:T(8,128)(2,1)S(1)} %pad_maximum_fusion.2), channel_id=1, source_target_pairs={{0,2},{2,4},{4,6},{6,8},{8,10},{10,12},{12,14},{14,16},{16,18},{18... | collective-permute-start | bytes 983048 | tf_op jit(solution)/shard_map/ppermute | solution.py:23
  53.1 1.2 copy-start
  148.4 1.2 copy-start.1
  149.7 116.0 %collective-permute-start.4 = (bf16[256,896]{1,0:T(8,128)(2,1)S(1)}, bf16[256,896]{1,0:T(8,128)(2,1)}, u32[]{:S(2)}, u32[]{:S(2)}) collective-permute-start(bf16[256,896]{1,0:T(8,128)(2,1)S(1)} %select_convert_fusion.1), channel_id=1, source_target_pairs={{0,1},{1,0},{2,3},{3,2},{4,5},{5,4},{6,7},{7,6},{8,9},{9,8},{10,11... | collective-permute-start | bytes 1376264 | tf_op jit(solution)/shard_map/ppermute | solution.py:132
  254.9 10.9 %copy-start.2 = (f32[256,1792]{1,0:T(8,128)S(1)}, f32[256,1792]{1,0:T(8,128)}, u32[]{:S(2)}) copy-start(f32[256,1792]{1,0:T(8,128)} %copy-done.1) | copy-start | bytes 5505028
  262.8 1.3 copy-start.3
  264.2 12.9 %copy-start.4 = (f32[256,1792]{1,0:T(8,128)S(1)}, f32[256,1792]{1,0:T(8,128)}, u32[]{:S(2)}) copy-start(f32[256,1792]{1,0:T(8,128)} %copy-done.3) | copy-start | bytes 5505028
  264.2 12.9 %collective-permute-start.5 = (bf16[256,896]{1,0:T(8,128)(2,1)S(1)}, bf16[256,896]{1,0:T(8,128)(2,1)}, u32[]{:S(2)}, u32[]{:S(2)}) collective-permute-start(bf16[256,896]{1,0:T(8,128)(2,1)S(1)} %select_convert_fusion), channel_id=1, source_target_pairs={{0,1},{1,0},{2,3},{3,2},{4,5},{5,4},{6,7},{7,6},{8,9},{9,8},{10,11... | collective-permute-start | bytes 1376264 | tf_op jit(solution)/shard_map/ppermute | solution.py:132
Sparse Core Ops, SparseCore 0:
  9.6 130.8 all-gather.2
  142.8 112.0 all-gather.4

commit v2 on v1

--- a/solution.py
+++ b/solution.py
@@ -16,6 +16,8 @@
 MARKS = 64
 FAR = 1e30
 PIECES = 2
+PLANE = 4
+PARTS = 2
 
 
 def from_behind(value, steps):
@@ -81,15 +83,9 @@
 
 
 def shards(q_nope, q_rope, latent, doc_ids, w_uk, w_uv, w_out):
-    rows = q_nope.shape[0]
-    count = lax.axis_size("seq")
+    count, heads = lax.axis_size("seq"), lax.axis_size("head")
     position = lax.axis_index("seq")
     w_rows = w_out.T
-    step = w_rows.shape[0] // PIECES
-    gathered = [
-        lax.all_gather(w_rows[i * step : (i + 1) * step], "seq", axis=0, tiled=True)
-        for i in range(PIECES)
-    ]
     marks = (doc_ids[:, None] == jnp.arange(MARKS, dtype=jnp.int32)[None, :]).astype(jnp.bfloat16)
     payload = jnp.concatenate([latent, marks], axis=1)
     blocks = []
@@ -110,26 +106,84 @@
     )
     q_mark = (marks - jnp.bfloat16(1)) * jnp.bfloat16(FAR)
     q_mark = jnp.concatenate([q_mark, q_mark], axis=1)
-    attended = attention(q_nope, q_rope, q_mark, content, tails, w_uk, w_uv)
-    heads = lax.axis_size("head")
-    mine = lax.axis_index("head")
-    swap = [(a, b) for a in range(heads) for b in range(heads) if a != b]
-    parts = []
-    for piece in gathered:
-        share = lax.dot_general(
-            attended, piece, (((1,), (1,)), ((), ())), preferred_element_type=jnp.float32
+    fixed = (q_mark, content, tails)
+    if count == 4 * PLANE and heads == 2:
+        return paired(w_rows, q_nope, q_rope, fixed, w_uk, w_uv)
+    attended = attention(q_nope, q_rope, *fixed, w_uk, w_uv)
+    whole = lax.all_gather(w_rows, "seq", axis=0, tiled=True)
+    share = product(attended, whole)
+    return lax.psum_scatter(share, "head", scatter_dimension=1, tiled=True).astype(jnp.bfloat16)
+
+
+def product(left, right):
+    return lax.dot_general(left, right, (((1,), (1,)), ((), ())), preferred_element_type=jnp.float32)
+
+
+def swapped(value, bit):
+    return lax.ppermute(value, "seq", [(i, i ^ bit) for i in range(lax.axis_size("seq"))])
+
+
+def spread(block, rank):
+    across = swapped(block, 2)
+    two = jnp.stack([block, across])
+    other = swapped(two, 1)
+    first = jnp.where(rank % 2 == 0, two, other)
+    second = jnp.where(rank % 2 == 0, other, two)
+    here, there = (first[0], second[0]), (first[1], second[1])
+    low = rank < 2
+    return jnp.concatenate(
+        [jnp.where(low, h, t) for h, t in zip(here, there)] + [jnp.where(low, t, h) for h, t in zip(here, there)], axis=0
+    )
+
+
+def to_owner(share, near):
+    pairs = []
+    for seq in range(lax.axis_size("seq")):
+        group = seq // (2 * PLANE)
+        keeper = group if near else 1 - group
+        pairs.append((2 * seq + 1 - keeper, 2 * seq + keeper))
+    return lax.ppermute(share.astype(jnp.bfloat16), ("seq", "head"), pairs).astype(jnp.float32)
+
+
+def paired(w_rows, q_nope, q_rope, fixed, w_uk, w_uv):
+    rows, width = q_nope.shape
+    position, mine = lax.axis_index("seq"), lax.axis_index("head")
+    plane, rank = position // PLANE, position % PLANE
+    slab = w_rows.shape[0]
+    step = slab // PIECES
+    near = spread(w_rows, rank)
+    far = [
+        spread(swapped(w_rows[i * step : (i + 1) * step], 2 * PLANE), rank) for i in range(PIECES)
+    ]
+    own, partner = [], []
+    for i in range(PARTS):
+        cut = width // PARTS
+        part = attention(
+            q_nope[:, i * cut : (i + 1) * cut],
+            q_rope[:, i * cut // 2 : (i + 1) * cut // 2],
+            *fixed,
+            w_uk[:, i * cut : (i + 1) * cut],
+            w_uv[:, i * cut : (i + 1) * cut],
         )
-        parts.append(lax.psum_scatter(share, "head", scatter_dimension=1, tiled=True) if heads > 2 else exchange(share, mine))
-    joined = jnp.stack([part.reshape(rows, count // heads, step) for part in parts], axis=2)
-    return joined.reshape(rows, -1).astype(jnp.bfloat16)
-
-
-def exchange(share, mine):
-    half = share.shape[1] // 2
-    first, second = share[:, :half], share[:, half:]
-    keep = jnp.where(mine == 0, first, second)
-    give = jnp.where(mine == 0, second, first).astype(jnp.bfloat16)
-    return keep + lax.ppermute(give, "head", [(0, 1), (1, 0)]).astype(jnp.float32)
+        own.append(part)
+        partner.append(swapped(part, PLANE))
+    own, partner = jnp.concatenate(own, axis=1), jnp.concatenate(partner, axis=1)
+    keeps_near = plane // 2 == mine
+
+    def finish(tokens):
+        share = product(tokens, near)
+        near_sum = share + to_owner(share, True)
+        far_sums = []
+        for piece in far:
+            share = product(tokens, piece)
+            far_sums.append((share + to_owner(share, False)).reshape(rows, PLANE, step))
+        far_sum = jnp.stack(far_sums, axis=2).reshape(rows, PLANE * slab)
+        return jnp.where(keeps_near, near_sum, far_sum).astype(jnp.bfloat16)
+
+    back = swapped(finish(partner), PLANE)
+    here = finish(own)
+    even = plane % 2 == 0
+    return jnp.concatenate([jnp.where(even, here, back), jnp.where(even, back, here)], axis=1)
 
 
 def solution(mesh):

time: 290 us -> 217 us (0.75)
  waiting for transfers between devices: 194 us -> 87.9 us
  starting transfers between devices: 15.3 us -> 42.2 us
  other arithmetic: 4.14 us -> 20.8 us
  between operations: 13.6 us -> 0.49 us
  local copies, waits for them, and re-layouts: 8.72 us -> 16.5 us
  matrix products: 15.8 us -> 12.5 us
    all_gather x2 -> x0, waiting for transfers between devices: 155 us -> none  [shards(): lax.all_gather(w_rows[i * step:(i + 1) * step], 'seq', axis=0, tiled=True)]
    ppermute x2 -> x17, waiting for transfers between devices: 9.92 us -> 87.9 us  [the longest x11 61.7 us: swapped(): lax.ppermute(value, 'seq', [(i, i ^ bit) for i in range(lax.axis_size('se...]
    ppermute x4, waiting for transfers between devices: 28.8 us -> 0.01 us  [from_behind(): lax.ppermute(value, 'seq', [(source, source + steps) for source in range(...]
    ppermute x2 -> x17, starting transfers between devices: 3.07 us -> 30 us  [the longest x11 16.7 us: swapped(): lax.ppermute(value, 'seq', [(i, i ^ bit) for i in range(lax.axis_size('se...]
    select_n x0 -> x8, other arithmetic: none -> 7.69 us  [the longest x3 5.35 us: spread(): first = jnp.where(rank % 2 == 0, two, other)]
    slice x1 -> x4, local copies, waits for them, and re-layouts: 2.96 us -> 10 us  [the longest x1 5.13 us: paired(): w_uv[:, i * cut:(i + 1) * cut]]
    another operation x3 -> x5, other arithmetic: 2.41 us -> 6.16 us  [the longest x3 6.07 us: spread(): two = jnp.stack([block, across])]
    dot_general x2 -> x6, matrix products: 15.8 us -> 12.5 us  [product(): lax.dot_general(left, right, (((1,), (1,)), ((), ())), preferred_element_...]
  transfers between devices with their start and end apart: 8 -> 21, of which waited for: 6 -> 7; matrix products, arithmetic and copies ran while one was open for 7% -> 20% of each run, Pallas kernels for 12% -> 17%
where the time goes in v2:
time: 217 us; the launch traced here: 216 us
  waiting for transfers between devices  87.9 us (41%)
  starting transfers between devices  42.2 us (19%)
  Pallas kernels  36.1 us (17%)
  other arithmetic  20.8 us (10%)
  local copies, waits for them, and re-layouts  16.5 us (8%)
  matrix products  12.5 us (6%)
    ppermute x11, waiting for transfers between devices, swapped(): lax.ppermute(value, 'seq', [(i, i ^ bit) for i in range(lax.axis_size('se...  61.7 us
    pallas_call x2, Pallas kernels, attention(): pl.pallas_call(functools.partial(attend, rows), out_shape=jax.ShapeDtypeS...  36.1 us
    ppermute x6, waiting for transfers between devices, to_owner(): lax.ppermute(share.astype(jnp.bfloat16), ('seq', 'head'), pairs)  26.2 us
    ppermute x11, starting transfers between devices, swapped(): lax.ppermute(value, 'seq', [(i, i ^ bit) for i in range(lax.axis_size('se...  16.7 us
    ppermute x6, starting transfers between devices, to_owner(): lax.ppermute(share.astype(jnp.bfloat16), ('seq', 'head'), pairs)  13.3 us
    dot_general x6, matrix products, product(): lax.dot_general(left, right, (((1,), (1,)), ((), ())), preferred_element_...  12.5 us
    ppermute x4, starting transfers between devices, from_behind(): lax.ppermute(value, 'seq', [(source, source + steps) for source in range(...  12.1 us
    another operation x3, other arithmetic, spread(): two = jnp.stack([block, across])  6.07 us
  transfers between devices with their start and end apart: 21, of which 7 were waited for; matrix products, arithmetic and copies ran while one was open for 20% of the time, Pallas kernels for 17%

profile of v2, /device:TPU:4, one launch (start us, length us, event | category | flops | bytes accessed | tf_op | source)
XLA Modules:
  0.0 216.5 jit_solution(142558998625108905)
XLA Ops:
  0.0 1.2 copy.13
  2.8 3.5 %collective-permute-start = (bf16[256,640]{1,0:T(8,128)(2,1)}, bf16[256,640]{1,0:T(8,128)(2,1)S(1)}, u32[]{:S(2)}, u32[]{:S(2)}) collective-permute-start(bf16[256,640]{1,0:T(8,128)(2,1)} %pad_maximum_fusion.20), channel_id=1, source_target_pairs={{0,8},{2,10},{4,12},{6,14},{8,16},{10,18},{12,20},{14,22},{16,24},... | collective-permute-start | bytes 983048 | tf_op jit(solution)/shard_map/ppermute | solution.py:25
  6.3 2.6 %collective-permute-start.1 = (bf16[256,640]{1,0:T(8,128)(2,1)}, bf16[256,640]{1,0:T(8,128)(2,1)S(1)}, u32[]{:S(2)}, u32[]{:S(2)}) collective-permute-start(bf16[256,640]{1,0:T(8,128)(2,1)} %pad_maximum_fusion.20), channel_id=1, source_target_pairs={{0,6},{2,8},{4,10},{6,12},{8,14},{10,16},{12,18},{14,20},{16,22},{... | collective-permute-start | bytes 983048 | tf_op jit(solution)/shard_map/ppermute | solution.py:25
  8.9 3.4 %collective-permute-start.2 = (bf16[256,640]{1,0:T(8,128)(2,1)}, bf16[256,640]{1,0:T(8,128)(2,1)S(1)}, u32[]{:S(2)}, u32[]{:S(2)}) collective-permute-start(bf16[256,640]{1,0:T(8,128)(2,1)} %pad_maximum_fusion.20), channel_id=1, source_target_pairs={{0,4},{2,6},{4,8},{6,10},{8,12},{10,14},{12,16},{14,18},{16,20},{1... | collective-permute-start | bytes 983048 | tf_op jit(solution)/shard_map/ppermute | solution.py:25
  12.3 2.6 %collective-permute-start.3 = (bf16[256,640]{1,0:T(8,128)(2,1)}, bf16[256,640]{1,0:T(8,128)(2,1)S(1)}, u32[]{:S(2)}, u32[]{:S(2)}) collective-permute-start(bf16[256,640]{1,0:T(8,128)(2,1)} %pad_maximum_fusion.20), channel_id=1, source_target_pairs={{0,2},{2,4},{4,6},{6,8},{8,10},{10,12},{12,14},{14,16},{16,18},{18... | collective-permute-start | bytes 983048 | tf_op jit(solution)/shard_map/ppermute | solution.py:25
  16.3 2.9 %fusion.16 = (bf16[112,4096]{1,0:T(8,128)(2,1)}, bf16[112,4096]{1,0:T(8,128)(2,1)}) fusion(bf16[224,4096]{1,0:T(8,128)(2,1)} %bitcast.58), kind=kLoop, calls=%fused_computation.70 | loop fusion | bytes 3670016 | tf_op jit(solution)/shard_map/slice | solution.py:156
  19.2 1.9 fusion.15
  21.1 0.9 copy-done.1
  22.0 5.1 %fusion.13 = (bf16[512,2048]{1,0:T(8,128)(2,1)}, bf16[512,2048]{1,0:T(8,128)(2,1)}, bf16[512,2048]{1,0:T(8,128)(2,1)}, bf16[512,2048]{1,0:T(8,128)(2,1)}) fusion(bf16[512,4096]{1,0:T(8,128)(2,1)S(1)} %copy-done.1, bf16[512,4096]{1,0:T(8,128)(2,1)} %param.11), kind=kLoop, calls=%fused_computation.67 | loop fusion | bytes 16777216 | tf_op jit(solution)/shard_map/slice | solution.py:166
  27.3 1.3 collective-permute-start.7
  28.8 1.8 collective-permute-start.11
  31.9 18.1 %attention.2 = bf16[256,2048]{1,0:T(8,128)(2,1)S(1)} custom-call(bf16[256,2048]{1,0:T(8,128)(2,1)S(1)} %get-tuple-element.22.q_nope, bf16[256,1024]{1,0:T(8,128)(2,1)S(1)} %get-tuple-element.36.q_rope, bf16[256,128]{1,0:T(8,128)(2,1)S(1)} %pad_maximum_fusion.21.q_mark, bf16[1280,512]{1,0:T(8,128)(2,1)S(1)} %slice.141.content, ...), custom_call_target="tpu_custom_call" | custom-call | flops 10737418240 | bytes 7340032 | tf_op jit(solution)/shard_map/attention/pallas_call | solution.py:59
  50.0 1.6 collective-permute-start.15
  51.6 39.4 %collective-permute-done.7 = bf16[112,4096]{1,0:T(8,128)(2,1)S(1)} collective-permute-done((bf16[112,4096]{1,0:T(8,128)(2,1)}, bf16[112,4096]{1,0:T(8,128)(2,1)S(1)}, u32[]{:S(2)}, u32[]{:S(2)}) %collective-permute-start.7) | collective-permute-done | bytes 917536 | tf_op jit(solution)/shard_map/ppermute | solution.py:123
  91.0 1.6 collective-permute-start.8
  92.6 18.1 %attention.3 = bf16[256,2048]{1,0:T(8,128)(2,1)S(1)} custom-call(bf16[256,2048]{1,0:T(8,128)(2,1)S(1)} %get-tuple-element.21.q_nope, bf16[256,1024]{1,0:T(8,128)(2,1)S(1)} %get-tuple-element.35.q_rope, bf16[256,128]{1,0:T(8,128)(2,1)S(1)} %pad_maximum_fusion.21.q_mark, bf16[1280,512]{1,0:T(8,128)(2,1)S(1)} %slice.141.content, ...), custom_call_target="tpu_custom_call" | custom-call | flops 10737418240 | bytes 7340032 | tf_op jit(solution)/shard_map/attention/pallas_call | solution.py:59
  110.7 2.5 %collective-permute-done.8 = bf16[112,4096]{1,0:T(8,128)(2,1)S(1)} collective-permute-done((bf16[112,4096]{1,0:T(8,128)(2,1)S(1)}, bf16[112,4096]{1,0:T(8,128)(2,1)S(1)}, u32[]{:S(2)}, u32[]{:S(2)}) %collective-permute-start.8) | collective-permute-done | bytes 917536 | tf_op jit(solution)/shard_map/ppermute | solution.py:123
  113.2 1.5 pad_maximum_fusion.5
  114.7 0.8 collective-permute-start.9
  115.6 1.7 collective-permute-start.12
  117.3 1.3 constant_dynamic-update-slice_fusion.2
  118.6 18.3 %collective-permute-done.16 = bf16[256,2048]{1,0:T(8,128)(2,1)} collective-permute-done((bf16[256,2048]{1,0:T(8,128)(2,1)S(1)}, bf16[256,2048]{1,0:T(8,128)(2,1)}, u32[]{:S(2)}, u32[]{:S(2)}) %collective-permute-start.16) | collective-permute-done | bytes 1048608 | tf_op jit(solution)/shard_map/ppermute | solution.py:123
  136.9 1.3 constant_dynamic-update-slice_fusion.1
  138.2 4.4 %pad_maximum_fusion.1 = bf16[2,224,4096]{2,1,0:T(8,128)(2,1)} fusion(bf16[1,224,4096]{2,1,0:T(8,128)(2,1)} %bitcast.4, bf16[1,224,4096]{2,1,0:T(8,128)(2,1)S(1)} %bitcast.60), kind=kLoop, calls=%fused_computation.1 | loop fusion | flops 1835008 | bytes 7340032 | tf_op jit(solution)/shard_map/stack | solution.py:128
  142.6 7.1 %collective-permute-start.5 = (bf16[2,224,4096]{2,1,0:T(8,128)(2,1)}, bf16[2,224,4096]{2,1,0:T(8,128)(2,1)}, u32[]{:S(2)}, u32[]{:S(2)}) collective-permute-start(bf16[2,224,4096]{2,1,0:T(8,128)(2,1)} %pad_maximum_fusion.1), channel_id=1, source_target_pairs={{0,2},{2,0},{4,6},{6,4},{8,10},{10,8},{12,14},{14,12},{16,18},{18,... | collective-permute-start | bytes 11010056 | tf_op jit(solution)/shard_map/ppermute | solution.py:123
  150.0 1.7 broadcast_select_fusion.5
  152.0 1.2 fusion.20
  153.1 3.6 %collective-permute-start.18 = (bf16[256,448]{0,1:T(8,128)(2,1)S(1)}, bf16[256,448]{0,1:T(8,128)(2,1)S(1)}, u32[]{:S(2)}, u32[]{:S(2)}) collective-permute-start(bf16[256,448]{0,1:T(8,128)(2,1)S(1)} %get-tuple-element.39), channel_id=1, source_target_pairs={{0,1},{2,3},{4,5},{6,7},{8,9},{10,11},{12,13},{14,15},{17,16},{19,... | collective-permute-start | bytes 688136 | tf_op jit(solution)/shard_map/ppermute | solution.py:145
  156.7 1.9 fusion.23
  159.1 1.1 fusion.19
  160.3 2.0 fusion.22
  162.3 3.8 %collective-permute-start.10 = (bf16[256,448]{0,1:T(8,128)(2,1)}, bf16[256,448]{0,1:T(8,128)(2,1)}, u32[]{:S(2)}, u32[]{:S(2)}) collective-permute-start(bf16[256,448]{0,1:T(8,128)(2,1)} %get-tuple-element.45), channel_id=1, source_target_pairs={{0,1},{2,3},{4,5},{6,7},{8,9},{10,11},{12,13},{14,15},{17,16},{19,... | collective-permute-start | bytes 688136 | tf_op jit(solution)/shard_map/ppermute | solution.py:145
  166.0 2.0 collective-permute-start.14
  168.0 1.3 collective-permute-start.19
  169.4 11.4 %collective-permute-done.19 = bf16[256,448]{0,1:T(8,128)(2,1)S(1)} collective-permute-done((bf16[256,448]{0,1:T(8,128)(2,1)S(1)}, bf16[256,448]{0,1:T(8,128)(2,1)S(1)}, u32[]{:S(2)}, u32[]{:S(2)}) %collective-permute-start.19) | collective-permute-done | bytes 229408 | tf_op jit(solution)/shard_map/ppermute | solution.py:145
  181.1 3.4 %broadcast_select_fusion.1 = (bf16[2,224,4096]{2,1,0:T(8,128)(2,1)S(1)}, bf16[2,224,4096]{2,1,0:T(8,128)(2,1)S(1)}) fusion(bf16[2,224,4096]{2,1,0:T(8,128)(2,1)} %collective-permute-done.5, pred[]{:T(512)S(6)} %eq.41, bf16[1,224,4096]{2,1,0:T(8,128)(2,1)} %bitcast.4, bf16[1,224,4096]{2,1,0:T(8,128)(2,1)} %bitcast.59), kind=kLoop, calls=%fused_computation.5 | loop fusion | flops 5505024 | bytes 14680065 | tf_op jit(solution)/shard_map/jit(_where)/select_n | solution.py:130
  185.1 1.0 copy-done.9
  186.1 2.6 %fusion.21 = (bf16[256,896]{1,0:T(8,128)(2,1)S(1)}, f32[256,896]{1,0:T(8,128)S(1)}) fusion(bf16[256,4096]{1,0:T(8,128)(2,1)S(1)} %copy-done.9, bf16[224,4096]{1,0:T(8,128)(2,1)S(1)} %get-tuple-element.16, bf16[224,4096]{1,0:T(8,128)(2,1)S(1)} %get-tuple-element.53, bf16[224,4096]{1,0:T(8,128)(2,1)S(1)} %get-tuple-element.15, ...), kind=kOutput, calls=%fused_computation.75 | convolution fusion | flops 1908637696 | bytes 10813440 | tf_op jit(solution)/shard_map/dot_general | solution.py:119
  188.7 1.3 collective-permute-start.17
  190.0 3.7 %fusion.24 = (bf16[256,896]{1,0:T(8,128)(2,1)}, f32[256,896]{1,0:T(8,128)}) fusion(bf16[224,4096]{1,0:T(8,128)(2,1)S(1)} %get-tuple-element.16, bf16[224,4096]{1,0:T(8,128)(2,1)S(1)} %get-tuple-element.53, bf16[224,4096]{1,0:T(8,128)(2,1)S(1)} %get-tuple-element.15, bf16[224,4096]{1,0:T(8,128)(2,1)S(1)} %get-tuple-element.54, ...), kind=kOutput, calls=%fused_computation.78 | convolution fusion | flops 1912832000 | bytes 10813440 | tf_op jit(solution)/shard_map/dot_general | solution.py:119
  193.7 1.4 collective-permute-start.6
  195.1 8.9 %collective-permute-done.17 = bf16[256,896]{1,0:T(8,128)(2,1)S(1)} collective-permute-done((bf16[256,896]{1,0:T(8,128)(2,1)S(1)}, bf16[256,896]{1,0:T(8,128)(2,1)S(1)}, u32[]{:S(2)}, u32[]{:S(2)}) %collective-permute-start.17) | collective-permute-done | bytes 458784 | tf_op jit(solution)/shard_map/ppermute | solution.py:145
  204.3 1.1 convert_add_fusion.3
  205.4 1.0 convert_add_fusion.2
  206.7 6.0 %collective-permute-done.6 = bf16[256,896]{1,0:T(8,128)(2,1)} collective-permute-done((bf16[256,896]{1,0:T(8,128)(2,1)}, bf16[256,896]{1,0:T(8,128)(2,1)}, u32[]{:S(2)}, u32[]{:S(2)}) %collective-permute-start.6) | collective-permute-done | bytes 458784 | tf_op jit(solution)/shard_map/ppermute | solution.py:145
  212.6 1.5 collective-permute-done.20
  214.2 1.2 broadcast_select_fusion.7
  215.5 1.0 pad_maximum_fusion.11
  (69 shorter events, 7.3 us)
Async XLA Ops:
  2.8 24.6 %collective-permute-start = (bf16[256,640]{1,0:T(8,128)(2,1)}, bf16[256,640]{1,0:T(8,128)(2,1)S(1)}, u32[]{:S(2)}, u32[]{:S(2)}) collective-permute-start(bf16[256,640]{1,0:T(8,128)(2,1)} %pad_maximum_fusion.20), channel_id=1, source_target_pairs={{0,8},{2,10},{4,12},{6,14},{8,16},{10,18},{12,20},{14,22},{16,24},... | collective-permute-start | bytes 983048 | tf_op jit(solution)/shard_map/ppermute | solution.py:25
  6.3 22.5 %collective-permute-start.1 = (bf16[256,640]{1,0:T(8,128)(2,1)}, bf16[256,640]{1,0:T(8,128)(2,1)S(1)}, u32[]{:S(2)}, u32[]{:S(2)}) collective-permute-start(bf16[256,640]{1,0:T(8,128)(2,1)} %pad_maximum_fusion.20), channel_id=1, source_target_pairs={{0,6},{2,8},{4,10},{6,12},{8,14},{10,16},{12,18},{14,20},{16,22},{... | collective-permute-start | bytes 983048 | tf_op jit(solution)/shard_map/ppermute | solution.py:25
  8.9 22.0 %collective-permute-start.2 = (bf16[256,640]{1,0:T(8,128)(2,1)}, bf16[256,640]{1,0:T(8,128)(2,1)S(1)}, u32[]{:S(2)}, u32[]{:S(2)}) collective-permute-start(bf16[256,640]{1,0:T(8,128)(2,1)} %pad_maximum_fusion.20), channel_id=1, source_target_pairs={{0,4},{2,6},{4,8},{6,10},{8,12},{10,14},{12,16},{14,18},{16,20},{1... | collective-permute-start | bytes 983048 | tf_op jit(solution)/shard_map/ppermute | solution.py:25
  12.3 18.8 %collective-permute-start.3 = (bf16[256,640]{1,0:T(8,128)(2,1)}, bf16[256,640]{1,0:T(8,128)(2,1)S(1)}, u32[]{:S(2)}, u32[]{:S(2)}) collective-permute-start(bf16[256,640]{1,0:T(8,128)(2,1)} %pad_maximum_fusion.20), channel_id=1, source_target_pairs={{0,2},{2,4},{4,6},{6,8},{8,10},{10,12},{12,14},{14,16},{16,18},{18... | collective-permute-start | bytes 983048 | tf_op jit(solution)/shard_map/ppermute | solution.py:25
  14.9 123.3 %collective-permute-start.4 = (bf16[224,4096]{1,0:T(8,128)(2,1)}, bf16[224,4096]{1,0:T(8,128)(2,1)}, u32[]{:S(2)}, u32[]{:S(2)}) collective-permute-start(bf16[224,4096]{1,0:T(8,128)(2,1)} %bitcast.57), channel_id=1, source_target_pairs={{0,4},{2,6},{4,0},{6,2},{8,12},{10,14},{12,8},{14,10},{16,20},{18,... | collective-permute-start | bytes 5505032 | tf_op jit(solution)/shard_map/ppermute | solution.py:123
  19.2 2.8 %copy-start.1 = (bf16[512,4096]{1,0:T(8,128)(2,1)S(1)}, bf16[512,4096]{1,0:T(8,128)(2,1)}, u32[]{:S(2)}) copy-start(bf16[512,4096]{1,0:T(8,128)(2,1)} %param.12) | copy-start | bytes 12582916
  22.0 5.2 %copy-start.6 = (bf16[256,2048]{1,0:T(8,128)(2,1)S(1)}, bf16[256,2048]{1,0:T(8,128)(2,1)}, u32[]{:S(2)}) copy-start(bf16[256,2048]{1,0:T(8,128)(2,1)} %param.8) | copy-start | bytes 3145732
  27.3 63.6 %collective-permute-start.7 = (bf16[112,4096]{1,0:T(8,128)(2,1)}, bf16[112,4096]{1,0:T(8,128)(2,1)S(1)}, u32[]{:S(2)}, u32[]{:S(2)}) collective-permute-start(bf16[112,4096]{1,0:T(8,128)(2,1)} %get-tuple-element.27), channel_id=1, source_target_pairs={{0,16},{2,18},{4,20},{6,22},{8,24},{10,26},{12,28},{14,30},{16,0},... | collective-permute-start | bytes 2752520 | tf_op jit(solution)/shard_map/ppermute | solution.py:123
  28.8 86.8 %collective-permute-start.11 = (bf16[112,4096]{1,0:T(8,128)(2,1)}, bf16[112,4096]{1,0:T(8,128)(2,1)S(1)}, u32[]{:S(2)}, u32[]{:S(2)}) collective-permute-start(bf16[112,4096]{1,0:T(8,128)(2,1)} %get-tuple-element.28), channel_id=1, source_target_pairs={{0,16},{2,18},{4,20},{6,22},{8,24},{10,26},{12,28},{14,30},{16,0},... | collective-permute-start | bytes 2752520 | tf_op jit(solution)/shard_map/ppermute | solution.py:123
  50.0 67.3 %collective-permute-start.15 = (bf16[256,2048]{1,0:T(8,128)(2,1)S(1)}, bf16[256,2048]{1,0:T(8,128)(2,1)}, u32[]{:S(2)}, u32[]{:S(2)}) collective-permute-start(bf16[256,2048]{1,0:T(8,128)(2,1)S(1)} %attention.2), channel_id=1, source_target_pairs={{0,8},{2,10},{4,12},{6,14},{8,0},{10,2},{12,4},{14,6},{16,24},{18,... | collective-permute-start | bytes 3145736 | tf_op jit(solution)/shard_map/ppermute | solution.py:123
  91.0 22.2 %copy-start.2 = (bf16[112,4096]{1,0:T(8,128)(2,1)}, bf16[112,4096]{1,0:T(8,128)(2,1)S(1)}, u32[]{:S(2)}) copy-start(bf16[112,4096]{1,0:T(8,128)(2,1)S(1)} %collective-permute-done.7) | copy-start | bytes 2752516
  91.0 22.2 %collective-permute-start.8 = (bf16[112,4096]{1,0:T(8,128)(2,1)S(1)}, bf16[112,4096]{1,0:T(8,128)(2,1)S(1)}, u32[]{:S(2)}, u32[]{:S(2)}) collective-permute-start(bf16[112,4096]{1,0:T(8,128)(2,1)S(1)} %collective-permute-done.7), channel_id=1, source_target_pairs={{0,4},{2,6},{4,0},{6,2},{8,12},{10,14},{12,8},{14,10},{16,20},{18,... | collective-permute-start | bytes 2752520 | tf_op jit(solution)/shard_map/ppermute | solution.py:123
  110.6 26.3 %collective-permute-start.16 = (bf16[256,2048]{1,0:T(8,128)(2,1)S(1)}, bf16[256,2048]{1,0:T(8,128)(2,1)}, u32[]{:S(2)}, u32[]{:S(2)}) collective-permute-start(bf16[256,2048]{1,0:T(8,128)(2,1)S(1)} %attention.3), channel_id=1, source_target_pairs={{0,8},{2,10},{4,12},{6,14},{8,0},{10,2},{12,4},{14,6},{16,24},{18,... | collective-permute-start | bytes 3145736 | tf_op jit(solution)/shard_map/ppermute | solution.py:123
  113.2 1.5 copy-start.4
  114.7 35.2 %collective-permute-start.9 = (bf16[2,112,4096]{2,1,0:T(8,128)(2,1)}, bf16[2,112,4096]{2,1,0:T(8,128)(2,1)}, u32[]{:S(2)}, u32[]{:S(2)}) collective-permute-start(bf16[2,112,4096]{2,1,0:T(8,128)(2,1)} %pad_maximum_fusion.5), channel_id=1, source_target_pairs={{0,2},{2,0},{4,6},{6,4},{8,10},{10,8},{12,14},{14,12},{16,18},{18,... | collective-permute-start | bytes 5505032 | tf_op jit(solution)/shard_map/ppermute | solution.py:123
  115.6 22.7 %copy-start = (bf16[4096,224]{0,1:T(8,128)(2,1)S(1)}, bf16[4096,224]{0,1:T(8,128)(2,1)}, u32[]{:S(2)}) copy-start(bf16[4096,224]{0,1:T(8,128)(2,1)} %param.13) | copy-start | bytes 5505028
  115.6 34.1 %collective-permute-start.12 = (bf16[112,4096]{1,0:T(8,128)(2,1)S(1)}, bf16[112,4096]{1,0:T(8,128)(2,1)S(1)}, u32[]{:S(2)}, u32[]{:S(2)}) collective-permute-start(bf16[112,4096]{1,0:T(8,128)(2,1)S(1)} %collective-permute-done.11), channel_id=1, source_target_pairs={{0,4},{2,6},{4,0},{6,2},{8,12},{10,14},{12,8},{14,10},{16,20},{18,... | collective-permute-start | bytes 2752520 | tf_op jit(solution)/shard_map/ppermute | solution.py:123
  138.2 20.9 %copy-start.8 = (bf16[256,4096]{1,0:T(8,128)(2,1)}, bf16[256,4096]{1,0:T(8,128)(2,1)S(1)}, u32[]{:S(2)}) copy-start(bf16[256,4096]{1,0:T(8,128)(2,1)S(1)} %constant_dynamic-update-slice_fusion.1) | copy-start | bytes 6291460
  142.6 7.4 %copy-start.3 = (bf16[112,4096]{1,0:T(8,128)(2,1)S(1)}, bf16[112,4096]{1,0:T(8,128)(2,1)}, u32[]{:S(2)}) copy-start(bf16[112,4096]{1,0:T(8,128)(2,1)} %copy-done.2) | copy-start | bytes 2752516
  142.6 7.4 %copy-start.5 = (bf16[112,4096]{1,0:T(8,128)(2,1)S(1)}, bf16[112,4096]{1,0:T(8,128)(2,1)}, u32[]{:S(2)}) copy-start(bf16[112,4096]{1,0:T(8,128)(2,1)} %copy-done.4) | copy-start | bytes 2752516
  142.6 38.5 %collective-permute-start.5 = (bf16[2,224,4096]{2,1,0:T(8,128)(2,1)}, bf16[2,224,4096]{2,1,0:T(8,128)(2,1)}, u32[]{:S(2)}, u32[]{:S(2)}) collective-permute-start(bf16[2,224,4096]{2,1,0:T(8,128)(2,1)} %pad_maximum_fusion.1), channel_id=1, source_target_pairs={{0,2},{2,0},{4,6},{6,4},{8,10},{10,8},{12,14},{14,12},{16,18},{18,... | collective-permute-start | bytes 11010056 | tf_op jit(solution)/shard_map/ppermute | solution.py:123
  149.9 8.7 %collective-permute-start.13 = (bf16[2,112,4096]{2,1,0:T(8,128)(2,1)S(1)}, bf16[2,112,4096]{2,1,0:T(8,128)(2,1)S(1)}, u32[]{:S(2)}, u32[]{:S(2)}) collective-permute-start(bf16[2,112,4096]{2,1,0:T(8,128)(2,1)S(1)} %pad_maximum_fusion.6), channel_id=1, source_target_pairs={{0,2},{2,0},{4,6},{6,4},{8,10},{10,8},{12,14},{14,12},{16,18},{18,... | collective-permute-start | bytes 5505032 | tf_op jit(solution)/shard_map/ppermute | solution.py:123
  153.1 16.2 %collective-permute-start.18 = (bf16[256,448]{0,1:T(8,128)(2,1)S(1)}, bf16[256,448]{0,1:T(8,128)(2,1)S(1)}, u32[]{:S(2)}, u32[]{:S(2)}) collective-permute-start(bf16[256,448]{0,1:T(8,128)(2,1)S(1)} %get-tuple-element.39), channel_id=1, source_target_pairs={{0,1},{2,3},{4,5},{6,7},{8,9},{10,11},{12,13},{14,15},{17,16},{19,... | collective-permute-start | bytes 688136 | tf_op jit(solution)/shard_map/ppermute | solution.py:145
  162.3 42.0 %collective-permute-start.10 = (bf16[256,448]{0,1:T(8,128)(2,1)}, bf16[256,448]{0,1:T(8,128)(2,1)}, u32[]{:S(2)}, u32[]{:S(2)}) collective-permute-start(bf16[256,448]{0,1:T(8,128)(2,1)} %get-tuple-element.45), channel_id=1, source_target_pairs={{0,1},{2,3},{4,5},{6,7},{8,9},{10,11},{12,13},{14,15},{17,16},{19,... | collective-permute-start | bytes 688136 | tf_op jit(solution)/shard_map/ppermute | solution.py:145
  166.0 39.3 %collective-permute-start.14 = (bf16[256,448]{0,1:T(8,128)(2,1)}, bf16[256,448]{0,1:T(8,128)(2,1)}, u32[]{:S(2)}, u32[]{:S(2)}) collective-permute-start(bf16[256,448]{0,1:T(8,128)(2,1)} %get-tuple-element.43), channel_id=1, source_target_pairs={{0,1},{2,3},{4,5},{6,7},{8,9},{10,11},{12,13},{14,15},{17,16},{19,... | collective-permute-start | bytes 688136 | tf_op jit(solution)/shard_map/ppermute | solution.py:145
  168.0 12.7 %collective-permute-start.19 = (bf16[256,448]{0,1:T(8,128)(2,1)S(1)}, bf16[256,448]{0,1:T(8,128)(2,1)S(1)}, u32[]{:S(2)}, u32[]{:S(2)}) collective-permute-start(bf16[256,448]{0,1:T(8,128)(2,1)S(1)} %get-tuple-element.37), channel_id=1, source_target_pairs={{0,1},{2,3},{4,5},{6,7},{8,9},{10,11},{12,13},{14,15},{17,16},{19,... | collective-permute-start | bytes 688136 | tf_op jit(solution)/shard_map/ppermute | solution.py:145
  184.5 1.6 copy-start.9
  188.7 15.3 %collective-permute-start.17 = (bf16[256,896]{1,0:T(8,128)(2,1)S(1)}, bf16[256,896]{1,0:T(8,128)(2,1)S(1)}, u32[]{:S(2)}, u32[]{:S(2)}) collective-permute-start(bf16[256,896]{1,0:T(8,128)(2,1)S(1)} %get-tuple-element.41), channel_id=1, source_target_pairs={{1,0},{3,2},{5,4},{7,6},{9,8},{11,10},{13,12},{15,14},{16,17},{18,... | collective-permute-start | bytes 1376264 | tf_op jit(solution)/shard_map/ppermute | solution.py:145
  193.7 11.7 %copy-start.10 = (f32[256,448]{0,1:T(8,128)S(1)}, f32[256,448]{0,1:T(8,128)}, u32[]{:S(2)}) copy-start(f32[256,448]{0,1:T(8,128)} %get-tuple-element.44) | copy-start | bytes 1376260
  193.7 18.9 %collective-permute-start.6 = (bf16[256,896]{1,0:T(8,128)(2,1)}, bf16[256,896]{1,0:T(8,128)(2,1)}, u32[]{:S(2)}, u32[]{:S(2)}) collective-permute-start(bf16[256,896]{1,0:T(8,128)(2,1)} %get-tuple-element.47), channel_id=1, source_target_pairs={{1,0},{3,2},{5,4},{7,6},{9,8},{11,10},{13,12},{15,14},{16,17},{18,... | collective-permute-start | bytes 1376264 | tf_op jit(solution)/shard_map/ppermute | solution.py:145
  204.2 10.0 %copy-start.7 = (f32[256,896]{1,0:T(8,128)S(1)}, f32[256,896]{1,0:T(8,128)}, u32[]{:S(2)}) copy-start(f32[256,896]{1,0:T(8,128)} %get-tuple-element.48) | copy-start | bytes 2752516
  204.2 10.0 %collective-permute-start.20 = (bf16[256,896]{1,0:T(8,128)(2,1)S(1)}, bf16[256,896]{1,0:T(8,128)(2,1)S(1)}, u32[]{:S(2)}, u32[]{:S(2)}) collective-permute-start(bf16[256,896]{1,0:T(8,128)(2,1)S(1)} %select_convert_fusion), channel_id=1, source_target_pairs={{0,8},{2,10},{4,12},{6,14},{8,0},{10,2},{12,4},{14,6},{16,24},{18,... | collective-permute-start | bytes 1376264 | tf_op jit(solution)/shard_map/ppermute | solution.py:123

commit v3 on v2

--- a/solution.py
+++ b/solution.py
@@ -17,7 +17,8 @@
 FAR = 1e30
 PIECES = 2
 PLANE = 4
-PARTS = 2
+PARTS = 4
+COST = 1 << 20
 
 
 def from_behind(value, steps):
@@ -51,33 +52,29 @@
         out[:, cols] = (total[:, :VD] / total[:, VD:]).astype(jnp.bfloat16)
 
 
-def attention(q_nope, q_rope, q_mark, content, tails, w_uk, w_uv):
-    rows, width = q_nope.shape
+def attention(start, pairs, q_nope, q_rope, q_mark, content, tails, w_uk, w_uv):
+    rows = q_nope.shape[0]
+    width = 2 * HD * pairs
     keys = content.shape[0]
-    pairs = width // (2 * HD)
     whole = lambda *shape: pl.BlockSpec(shape, lambda i: (0,) * len(shape))
     return pl.pallas_call(
         functools.partial(attend, rows),
         out_shape=jax.ShapeDtypeStruct((rows, width), jnp.bfloat16),
         grid=(pairs,),
         in_specs=[
-            pl.BlockSpec((rows, 2 * HD), lambda i: (0, i)),
-            pl.BlockSpec((rows, 2 * ROPE), lambda i: (0, i)),
+            pl.BlockSpec((rows, 2 * HD), lambda i: (0, i + start)),
+            pl.BlockSpec((rows, 2 * ROPE), lambda i: (0, i + start)),
             whole(rows, 2 * ROPE),
             whole(keys, LAT),
             whole(2, keys, 2 * ROPE),
-            pl.BlockSpec((LAT, 2 * HD), lambda i: (0, i)),
-            pl.BlockSpec((LAT, 2 * HD), lambda i: (0, i)),
+            pl.BlockSpec((LAT, 2 * HD), lambda i: (0, i + start)),
+            pl.BlockSpec((LAT, 2 * HD), lambda i: (0, i + start)),
         ],
         out_specs=pl.BlockSpec((rows, 2 * VD), lambda i: (0, i)),
         compiler_params=pltpu.CompilerParams(
             dimension_semantics=("arbitrary",), vmem_limit_bytes=48 << 20
         ),
-        cost_estimate=pl.CostEstimate(
-            flops=pairs * 2 * keys * (2 * LAT * 2 * HD + 4 * rows * 2 * HD),
-            bytes_accessed=2 * (rows * width * 3 + LAT * width * 2),
-            transcendentals=pairs * 2 * rows * keys,
-        ),
+        cost_estimate=pl.CostEstimate(flops=COST, bytes_accessed=COST, transcendentals=0),
         name="attention",
     )(q_nope, q_rope, q_mark, content, tails, w_uk, w_uv)
 
@@ -109,7 +106,7 @@
     fixed = (q_mark, content, tails)
     if count == 4 * PLANE and heads == 2:
         return paired(w_rows, q_nope, q_rope, fixed, w_uk, w_uv)
-    attended = attention(q_nope, q_rope, *fixed, w_uk, w_uv)
+    attended = attention(0, q_nope.shape[1] // (2 * HD), q_nope, q_rope, *fixed, w_uk, w_uv)
     whole = lax.all_gather(w_rows, "seq", axis=0, tiled=True)
     share = product(attended, whole)
     return lax.psum_scatter(share, "head", scatter_dimension=1, tiled=True).astype(jnp.bfloat16)
@@ -123,26 +120,32 @@
     return lax.ppermute(value, "seq", [(i, i ^ bit) for i in range(lax.axis_size("seq"))])
 
 
-def spread(block, rank):
-    across = swapped(block, 2)
-    two = jnp.stack([block, across])
-    other = swapped(two, 1)
-    first = jnp.where(rank % 2 == 0, two, other)
-    second = jnp.where(rank % 2 == 0, other, two)
-    here, there = (first[0], second[0]), (first[1], second[1])
-    low = rank < 2
-    return jnp.concatenate(
-        [jnp.where(low, h, t) for h, t in zip(here, there)] + [jnp.where(low, t, h) for h, t in zip(here, there)], axis=0
-    )
-
-
-def to_owner(share, near):
+def after(value, *earlier):
+    return lax.optimization_barrier((value, *earlier))[0]
+
+
+def pair_up(block, across):
+    two = jnp.concatenate([block, across], axis=0)
+    return two, swapped(two, 1)
+
+
+def owners(near):
     pairs = []
     for seq in range(lax.axis_size("seq")):
         group = seq // (2 * PLANE)
         keeper = group if near else 1 - group
-        pairs.append((2 * seq + 1 - keeper, 2 * seq + keeper))
+        pairs.append((seq, keeper))
+    return pairs
+
+
+def to_owner(share, near):
+    pairs = [(2 * seq + 1 - keeper, 2 * seq + keeper) for seq, keeper in owners(near)]
     return lax.ppermute(share.astype(jnp.bfloat16), ("seq", "head"), pairs).astype(jnp.float32)
+
+
+def to_tokens(done, near):
+    pairs = [(2 * seq + keeper, 2 * (seq ^ PLANE) + keeper) for seq, keeper in owners(near)]
+    return lax.ppermute(done, ("seq", "head"), pairs)
 
 
 def paired(w_rows, q_nope, q_rope, fixed, w_uk, w_uv):
@@ -151,39 +154,52 @@
     plane, rank = position // PLANE, position % PLANE
     slab = w_rows.shape[0]
     step = slab // PIECES
-    near = spread(w_rows, rank)
-    far = [
-        spread(swapped(w_rows[i * step : (i + 1) * step], 2 * PLANE), rank) for i in range(PIECES)
-    ]
-    own, partner = [], []
-    for i in range(PARTS):
-        cut = width // PARTS
-        part = attention(
-            q_nope[:, i * cut : (i + 1) * cut],
-            q_rope[:, i * cut // 2 : (i + 1) * cut // 2],
-            *fixed,
-            w_uk[:, i * cut : (i + 1) * cut],
-            w_uv[:, i * cut : (i + 1) * cut],
-        )
-        own.append(part)
-        partner.append(swapped(part, PLANE))
+    q_mark, content, tails = fixed
+    w_rows = lax.optimization_barrier(w_rows)
+    pieces = [w_rows[i * step : (i + 1) * step] for i in range(PIECES)]
+    far = [swapped(pieces[0], 2 * PLANE)]
+    near_across = swapped(w_rows, 2)
+    each = width // (2 * HD) // PARTS
+
+    def part(i, mark):
+        return attention(i * each, each, q_nope, q_rope, mark, content, tails, w_uk, w_uv)
+
+    own = [part(0, q_mark)]
+    far.append(swapped(after(pieces[1], own[0]), 2 * PLANE))
+    partner = [swapped(own[0], PLANE)]
+    own.append(part(1, after(q_mark, own[0])))
+    partner.append(swapped(own[1], PLANE))
+    own.append(part(2, after(q_mark, own[1], near_across)))
+    partner.append(swapped(own[2], PLANE))
+    near_pair = pair_up(w_rows, near_across)
+    own.append(part(3, after(q_mark, own[2])))
+    partner.append(swapped(own[3], PLANE))
+    far = [after(block, own[3]) for block in far]
     own, partner = jnp.concatenate(own, axis=1), jnp.concatenate(partner, axis=1)
+
+    def finish(pair, near, gate):
+        both = [jnp.concatenate([product(t, pair[0]), product(t, pair[1])], axis=1) for t in gate]
+        sums = [(share + to_owner(share, near)).astype(jnp.bfloat16) for share in both]
+        return both, sums[0], to_tokens(sums[1], near)
+
+    shares, near_own, near_back = finish(near_pair, True, (own, partner))
+    last = shares[1]
+    far_own, far_back = [], []
+    for piece, block in zip(pieces, far):
+        pair = pair_up(block, swapped(block, 2))
+        shares, one, two = finish(pair, False, (after(own, last), after(partner, last)))
+        last = shares[1]
+        far_own.append(one.reshape(rows, PLANE, 1, step))
+        far_back.append(two.reshape(rows, PLANE, 1, step))
     keeps_near = plane // 2 == mine
-
-    def finish(tokens):
-        share = product(tokens, near)
-        near_sum = share + to_owner(share, True)
-        far_sums = []
-        for piece in far:
-            share = product(tokens, piece)
-            far_sums.append((share + to_owner(share, False)).reshape(rows, PLANE, step))
-        far_sum = jnp.stack(far_sums, axis=2).reshape(rows, PLANE * slab)
-        return jnp.where(keeps_near, near_sum, far_sum).astype(jnp.bfloat16)
-
-    back = swapped(finish(partner), PLANE)
-    here = finish(own)
+    here = jnp.where(keeps_near, near_own.reshape(rows, PLANE, PIECES, step), jnp.concatenate(far_own, axis=2))
+    back = jnp.where(keeps_near, near_back.reshape(rows, PLANE, PIECES, step), jnp.concatenate(far_back, axis=2))
     even = plane % 2 == 0
-    return jnp.concatenate([jnp.where(even, here, back), jnp.where(even, back, here)], axis=1)
+    both = jnp.stack([jnp.where(even, here, back), jnp.where(even, back, here)], axis=1)
+    both = both.reshape(rows, 2, 2, 2, slab)
+    both = jnp.where(rank % 2 == 0, both, both[:, :, ::-1])
+    both = jnp.where(rank // 2 == 0, both, both[:, :, :, ::-1])
+    return both.transpose(0, 1, 3, 2, 4).reshape(rows, 2 * PLANE * slab)
 
 
 def solution(mesh):

time: 217 us -> 227 us (1.046)
  starting transfers between devices: 42.2 us -> 91.2 us
  waiting for transfers between devices: 87.9 us -> 57.8 us
  other arithmetic: 20.8 us -> 5.58 us
  matrix products: 12.5 us -> 18 us
  local copies, waits for them, and re-layouts: 16.5 us -> 13 us
  Pallas kernels: 36.1 us -> 38.7 us
    ppermute x11 -> x12, starting transfers between devices: 16.7 us -> 58 us  [swapped(): lax.ppermute(value, 'seq', [(i, i ^ bit) for i in range(lax.axis_size('se...]
    ppermute x11 -> x12, waiting for transfers between devices: 61.7 us -> 32.4 us  [swapped(): lax.ppermute(value, 'seq', [(i, i ^ bit) for i in range(lax.axis_size('se...]
    ppermute x6, waiting for transfers between devices: 26.2 us -> 7.42 us  [to_owner(): lax.ppermute(share.astype(jnp.bfloat16), ('seq', 'head'), pairs)]
    ppermute x0 -> x3, waiting for transfers between devices: none -> 9.82 us  [to_tokens(): return lax.ppermute(done, ('seq', 'head'), pairs)]
    ppermute x4, waiting for transfers between devices: 0.01 us -> 8.17 us  [from_behind(): lax.ppermute(value, 'seq', [(source, source + steps) for source in range(...]
    slice x4 -> x1, local copies, waits for them, and re-layouts: 10 us -> 2.86 us  [paired(): pieces = [w_rows[i * step:(i + 1) * step] for i in range(PIECES)]]
    select_n x7 -> x1, other arithmetic: 6.45 us -> 0.16 us  [paired(): both = jnp.where(rank % 2 == 0, both, both[:, :, ::-1])]
    another operation x5 -> x1, other arithmetic: 6.16 us -> 0.09 us  [paired(): jnp.stack([jnp.where(even, here, back), jnp.where(even, back, here)], axi...]
  transfers between devices with their start and end apart: 21 -> 25, of which waited for: 7 -> 9; matrix products, arithmetic and copies ran while one was open for 20% -> 12% of each run, Pallas kernels for 17% -> 17%
where the time goes in v3:
time: 227 us; the launch traced here: 225 us
  starting transfers between devices  91.2 us (40%)
  waiting for transfers between devices  57.8 us (25%)
  Pallas kernels  38.7 us (17%)
  matrix products  18 us (8%)
  local copies, waits for them, and re-layouts  13 us (6%)
  other arithmetic  5.58 us (2%)
    ppermute x12, starting transfers between devices, swapped(): lax.ppermute(value, 'seq', [(i, i ^ bit) for i in range(lax.axis_size('se...  58 us
    pallas_call x4, Pallas kernels, attention(): pl.pallas_call(functools.partial(attend, rows), out_shape=jax.ShapeDtypeS...  38.7 us
    ppermute x12, waiting for transfers between devices, swapped(): lax.ppermute(value, 'seq', [(i, i ^ bit) for i in range(lax.axis_size('se...  32.4 us
    dot_general x12, matrix products, product(): lax.dot_general(left, right, (((1,), (1,)), ((), ())), preferred_element_...  18 us
    ppermute x6, starting transfers between devices, to_owner(): lax.ppermute(share.astype(jnp.bfloat16), ('seq', 'head'), pairs)  17.4 us
    ppermute x4, starting transfers between devices, from_behind(): lax.ppermute(value, 'seq', [(source, source + steps) for source in range(...  12.1 us
    ppermute x3, waiting for transfers between devices, to_tokens(): return lax.ppermute(done, ('seq', 'head'), pairs)  9.82 us
    unnamed x24, local copies, waits for them, and re-layouts  8.31 us
  transfers between devices with their start and end apart: 25, of which 9 were waited for; matrix products, arithmetic and copies ran while one was open for 12% of the time, Pallas kernels for 17%

profile of v3, /device:TPU:4, one launch (start us, length us, event | category | flops | bytes accessed | tf_op | source)
XLA Modules:
  0.0 225.0 jit_solution(9092977366400413166)
XLA Ops:
  0.8 1.2 copy.16
  2.1 3.5 %collective-permute-start = (bf16[256,640]{1,0:T(8,128)(2,1)S(1)}, bf16[256,640]{1,0:T(8,128)(2,1)S(1)}, u32[]{:S(2)}, u32[]{:S(2)}) collective-permute-start(bf16[256,640]{1,0:T(8,128)(2,1)S(1)} %pad_maximum_fusion.12), channel_id=1, source_target_pairs={{0,8},{2,10},{4,12},{6,14},{8,16},{10,18},{12,20},{14,22},{16,24},... | collective-permute-start | bytes 983048 | tf_op jit(solution)/shard_map/ppermute | solution.py:26
  5.6 2.6 %collective-permute-start.1 = (bf16[256,640]{1,0:T(8,128)(2,1)S(1)}, bf16[256,640]{1,0:T(8,128)(2,1)S(1)}, u32[]{:S(2)}, u32[]{:S(2)}) collective-permute-start(bf16[256,640]{1,0:T(8,128)(2,1)S(1)} %pad_maximum_fusion.12), channel_id=1, source_target_pairs={{0,6},{2,8},{4,10},{6,12},{8,14},{10,16},{12,18},{14,20},{16,22},{... | collective-permute-start | bytes 983048 | tf_op jit(solution)/shard_map/ppermute | solution.py:26
  8.2 3.4 %collective-permute-start.2 = (bf16[256,640]{1,0:T(8,128)(2,1)S(1)}, bf16[256,640]{1,0:T(8,128)(2,1)S(1)}, u32[]{:S(2)}, u32[]{:S(2)}) collective-permute-start(bf16[256,640]{1,0:T(8,128)(2,1)S(1)} %pad_maximum_fusion.12), channel_id=1, source_target_pairs={{0,4},{2,6},{4,8},{6,10},{8,12},{10,14},{12,16},{14,18},{16,20},{1... | collective-permute-start | bytes 983048 | tf_op jit(solution)/shard_map/ppermute | solution.py:26
  11.6 2.6 %collective-permute-start.3 = (bf16[256,640]{1,0:T(8,128)(2,1)S(1)}, bf16[256,640]{1,0:T(8,128)(2,1)S(1)}, u32[]{:S(2)}, u32[]{:S(2)}) collective-permute-start(bf16[256,640]{1,0:T(8,128)(2,1)S(1)} %pad_maximum_fusion.12), channel_id=1, source_target_pairs={{0,2},{2,4},{4,6},{6,8},{8,10},{10,12},{12,14},{14,16},{16,18},{18... | collective-permute-start | bytes 983048 | tf_op jit(solution)/shard_map/ppermute | solution.py:26
  14.8 2.9 %fusion.10 = (bf16[112,4096]{1,0:T(8,128)(2,1)}, bf16[112,4096]{1,0:T(8,128)(2,1)}) fusion(bf16[224,4096]{1,0:T(8,128)(2,1)} %bitcast.51), kind=kLoop, calls=%fused_computation.57 | loop fusion | bytes 3670016 | tf_op jit(solution)/shard_map/slice | solution.py:159
  17.9 1.3 collective-permute-start.11
  19.4 1.4 collective-permute-done.1
  20.9 6.8 %collective-permute-done.2 = bf16[256,640]{1,0:T(8,128)(2,1)S(1)} collective-permute-done((bf16[256,640]{1,0:T(8,128)(2,1)S(1)}, bf16[256,640]{1,0:T(8,128)(2,1)S(1)}, u32[]{:S(2)}, u32[]{:S(2)}) %collective-permute-start.2) | collective-permute-done | bytes 327712 | tf_op jit(solution)/shard_map/ppermute | solution.py:26
  28.9 1.1 copy-done
  30.2 9.7 %attention.4 = bf16[256,1024]{1,0:T(8,128)(2,1)S(1)} custom-call(bf16[256,4096]{1,0:T(8,128)(2,1)S(1)} %copy-done, bf16[256,2048]{1,0:T(8,128)(2,1)S(1)} %copy-done.1, bf16[256,128]{1,0:T(8,128)(2,1)S(1)} %pad_maximum_fusion.13.q_mark, bf16[1280,512]{1,0:T(8,128)(2,1)S(1)} %slice.61.content, bf16[2,1280,128]{2,1,0:T(8,128)(2,1)S(1)} %pad_maximum_fusion.5.tails, ...), custom_call_target="tpu_custom_call" | custom-call | flops 1048576 | bytes 1048576 | tf_op jit(solution)/shard_map/attention/pallas_call | solution.py:60
  40.0 0.9 copy-done.5
  40.8 2.6 %collective-permute-start.15 = (bf16[112,4096]{1,0:T(8,128)(2,1)}, bf16[112,4096]{1,0:T(8,128)(2,1)}, u32[]{:S(2)}, u32[]{:S(2)}) collective-permute-start(bf16[112,4096]{1,0:T(8,128)(2,1)} %get-tuple-element.22), channel_id=1, source_target_pairs={{0,16},{2,18},{4,20},{6,22},{8,24},{10,26},{12,28},{14,30},{16,0},... | collective-permute-start | bytes 2752520 | tf_op jit(solution)/shard_map/ppermute | solution.py:120
  43.4 1.2 copy-done.2
  44.7 1.1 copy-done.4
  45.8 9.7 %attention.5 = bf16[256,1024]{1,0:T(8,128)(2,1)S(1)} custom-call(bf16[256,4096]{1,0:T(8,128)(2,1)S(1)} %copy-done, bf16[256,2048]{1,0:T(8,128)(2,1)S(1)} %copy-done.2, bf16[256,128]{1,0:T(8,128)(2,1)S(1)} %pad_maximum_fusion.13.q_mark, bf16[1280,512]{1,0:T(8,128)(2,1)S(1)} %slice.61.content, bf16[2,1280,128]{2,1,0:T(8,128)(2,1)S(1)} %copy-done.4, ...), custom_call_target="tpu_custom_call" | custom-call | flops 1048576 | bytes 1048576 | tf_op jit(solution)/shard_map/attention/pallas_call | solution.py:60
  55.4 2.1 collective-permute-start.8
  57.5 2.6 %collective-permute-done.4 = bf16[224,4096]{1,0:T(8,128)(2,1)} collective-permute-done((bf16[224,4096]{1,0:T(8,128)(2,1)}, bf16[224,4096]{1,0:T(8,128)(2,1)}, u32[]{:S(2)}, u32[]{:S(2)}) %collective-permute-start.4) | collective-permute-done | bytes 1835040 | tf_op jit(solution)/shard_map/ppermute | solution.py:120
  60.1 1.9 pad_maximum_fusion
  62.0 37.7 %collective-permute-start.5 = (bf16[448,4096]{1,0:T(8,128)(2,1)S(1)}, bf16[448,4096]{1,0:T(8,128)(2,1)}, u32[]{:S(2)}, u32[]{:S(2)}) collective-permute-start(bf16[448,4096]{1,0:T(8,128)(2,1)S(1)} %pad_maximum_fusion), channel_id=1, source_target_pairs={{0,2},{2,0},{4,6},{6,4},{8,10},{10,8},{12,14},{14,12},{16,18},{18,... | collective-permute-start | bytes 11010056 | tf_op jit(solution)/shard_map/ppermute | solution.py:120
  99.8 2.4 %collective-permute-done.8 = bf16[256,1024]{1,0:T(8,128)(2,1)S(1)} collective-permute-done((bf16[256,1024]{1,0:T(8,128)(2,1)S(1)}, bf16[256,1024]{1,0:T(8,128)(2,1)S(1)}, u32[]{:S(2)}, u32[]{:S(2)}) %collective-permute-start.8) | collective-permute-done | bytes 524320 | tf_op jit(solution)/shard_map/ppermute | solution.py:120
  102.3 9.6 %attention.6 = bf16[256,1024]{1,0:T(8,128)(2,1)S(1)} custom-call(bf16[256,4096]{1,0:T(8,128)(2,1)S(1)} %copy-done, bf16[256,2048]{1,0:T(8,128)(2,1)S(1)} %copy-done.2, bf16[256,128]{1,0:T(8,128)(2,1)S(1)} %pad_maximum_fusion.13.q_mark, bf16[1280,512]{1,0:T(8,128)(2,1)S(1)} %slice.61.content, bf16[2,1280,128]{2,1,0:T(8,128)(2,1)S(1)} %copy-done.4, ...), custom_call_target="tpu_custom_call" | custom-call | flops 1048576 | bytes 1048576 | tf_op jit(solution)/shard_map/attention/pallas_call | solution.py:60
  111.9 9.7 %attention.7 = bf16[256,1024]{1,0:T(8,128)(2,1)S(1)} custom-call(bf16[256,4096]{1,0:T(8,128)(2,1)S(1)} %copy-done, bf16[256,2048]{1,0:T(8,128)(2,1)S(1)} %copy-done.2, bf16[256,128]{1,0:T(8,128)(2,1)S(1)} %pad_maximum_fusion.13.q_mark, bf16[1280,512]{1,0:T(8,128)(2,1)S(1)} %slice.61.content, bf16[2,1280,128]{2,1,0:T(8,128)(2,1)S(1)} %copy-done.4, ...), custom_call_target="tpu_custom_call" | custom-call | flops 1048576 | bytes 1048576 | tf_op jit(solution)/shard_map/attention/pallas_call | solution.py:60
  121.7 2.1 collective-permute-start.10
  123.7 11.4 %collective-permute-start.12 = (bf16[112,4096]{1,0:T(8,128)(2,1)}, bf16[112,4096]{1,0:T(8,128)(2,1)S(1)}, u32[]{:S(2)}, u32[]{:S(2)}) collective-permute-start(bf16[112,4096]{1,0:T(8,128)(2,1)} %collective-permute-done.11), channel_id=1, source_target_pairs={{0,4},{2,6},{4,0},{6,2},{8,12},{10,14},{12,8},{14,10},{16,20},{18,... | collective-permute-start | bytes 2752520 | tf_op jit(solution)/shard_map/ppermute | solution.py:120
  135.3 1.2 constant_dynamic-update-slice_fusion.6
  136.7 2.6 %fusion.9 = f32[256,448]{0,1:T(8,128)S(1)} fusion(bf16[256,4096]{1,0:T(8,128)(2,1)S(1)} %pad_maximum_fusion.1, bf16[224,4096]{1,0:T(8,128)(2,1)} %collective-permute-done.4, bf16[224,4096]{1,0:T(8,128)(2,1)S(1)} %bitcast.53), kind=kOutput, calls=%fused_computation.56 | convolution fusion | flops 946864128 | bytes 6225920 | tf_op jit(solution)/shard_map/dot_general | solution.py:116
  139.4 1.2 constant_dynamic-update-slice_fusion.8
  140.7 16.0 %collective-permute-done.12 = bf16[112,4096]{1,0:T(8,128)(2,1)S(1)} collective-permute-done((bf16[112,4096]{1,0:T(8,128)(2,1)}, bf16[112,4096]{1,0:T(8,128)(2,1)S(1)}, u32[]{:S(2)}, u32[]{:S(2)}) %collective-permute-start.12) | collective-permute-done | bytes 917536 | tf_op jit(solution)/shard_map/ppermute | solution.py:120
  156.9 2.6 %fusion.8 = f32[256,448]{0,1:T(8,128)S(1)} fusion(bf16[256,4096]{1,0:T(8,128)(2,1)S(1)} %constant_dynamic-update-slice_fusion.1, bf16[224,4096]{1,0:T(8,128)(2,1)} %collective-permute-done.4, bf16[224,4096]{1,0:T(8,128)(2,1)S(1)} %bitcast.54), kind=kOutput, calls=%fused_computation.55 | convolution fusion | flops 946864128 | bytes 6225920 | tf_op jit(solution)/shard_map/dot_general | solution.py:116
  159.5 11.3 %collective-permute-done.16 = bf16[112,4096]{1,0:T(8,128)(2,1)S(1)} collective-permute-done((bf16[112,4096]{1,0:T(8,128)(2,1)}, bf16[112,4096]{1,0:T(8,128)(2,1)S(1)}, u32[]{:S(2)}, u32[]{:S(2)}) %collective-permute-start.16) | collective-permute-done | bytes 917536 | tf_op jit(solution)/shard_map/ppermute | solution.py:120
  171.0 3.2 %fusion.13 = f32[256,448]{0,1:T(8,128)S(1)} fusion(bf16[256,4096]{1,0:T(8,128)(2,1)S(1)} %constant_dynamic-update-slice_fusion.1, bf16[448,4096]{1,0:T(8,128)(2,1)} %collective-permute-done.5), kind=kOutput, calls=%fused_computation.60 | convolution fusion | flops 939524096 | bytes 6225920 | tf_op jit(solution)/shard_map/dot_general | solution.py:116
  174.3 1.3 collective-permute-start.19
  175.6 0.8 fusion.16
  177.2 4.6 %collective-permute-start.21 = (bf16[256,448]{0,1:T(8,128)(2,1)S(1)}, bf16[256,448]{0,1:T(8,128)(2,1)S(1)}, u32[]{:S(2)}, u32[]{:S(2)}) collective-permute-start(bf16[256,448]{0,1:T(8,128)(2,1)S(1)} %fusion.6), channel_id=1, source_target_pairs={{0,1},{2,3},{4,5},{6,7},{8,9},{10,11},{12,13},{14,15},{17,16},{19,... | collective-permute-start | bytes 688136 | tf_op jit(solution)/shard_map/ppermute | solution.py:143
  181.8 3.2 %fusion.12 = f32[256,448]{0,1:T(8,128)S(1)} fusion(bf16[256,4096]{1,0:T(8,128)(2,1)S(1)} %pad_maximum_fusion.1, bf16[448,4096]{1,0:T(8,128)(2,1)} %collective-permute-done.5), kind=kOutput, calls=%fused_computation.59 | convolution fusion | flops 939524096 | bytes 6225920 | tf_op jit(solution)/shard_map/dot_general | solution.py:116
  185.0 1.3 collective-permute-start.6
  186.3 0.8 fusion.18
  188.0 4.6 %collective-permute-start.18 = (bf16[256,448]{0,1:T(8,128)(2,1)S(1)}, bf16[256,448]{0,1:T(8,128)(2,1)S(1)}, u32[]{:S(2)}, u32[]{:S(2)}) collective-permute-start(bf16[256,448]{0,1:T(8,128)(2,1)S(1)} %fusion.3), channel_id=1, source_target_pairs={{0,1},{2,3},{4,5},{6,7},{8,9},{10,11},{12,13},{14,15},{17,16},{19,... | collective-permute-start | bytes 688136 | tf_op jit(solution)/shard_map/ppermute | solution.py:143
  193.3 0.8 fusion.20
  195.0 1.3 collective-permute-start.23
  196.3 0.8 fusion.15
  197.1 5.0 %collective-permute-done.23 = bf16[256,448]{0,1:T(8,128)(2,1)S(1)} collective-permute-done((bf16[256,448]{0,1:T(8,128)(2,1)S(1)}, bf16[256,448]{0,1:T(8,128)(2,1)S(1)}, u32[]{:S(2)}, u32[]{:S(2)}) %collective-permute-start.23) | collective-permute-done | bytes 229408 | tf_op jit(solution)/shard_map/ppermute | solution.py:143
  202.1 4.4 %collective-permute-start.14 = (bf16[256,448]{0,1:T(8,128)(2,1)S(1)}, bf16[256,448]{0,1:T(8,128)(2,1)S(1)}, u32[]{:S(2)}, u32[]{:S(2)}) collective-permute-start(bf16[256,448]{0,1:T(8,128)(2,1)S(1)} %fusion.4), channel_id=1, source_target_pairs={{0,1},{2,3},{4,5},{6,7},{8,9},{10,11},{12,13},{14,15},{17,16},{19,... | collective-permute-start | bytes 688136 | tf_op jit(solution)/shard_map/ppermute | solution.py:143
  208.1 2.4 %collective-permute-done.14 = bf16[256,448]{0,1:T(8,128)(2,1)S(1)} collective-permute-done((bf16[256,448]{0,1:T(8,128)(2,1)S(1)}, bf16[256,448]{0,1:T(8,128)(2,1)S(1)}, u32[]{:S(2)}, u32[]{:S(2)}) %collective-permute-start.14) | collective-permute-done | bytes 229408 | tf_op jit(solution)/shard_map/ppermute | solution.py:143
  210.7 2.3 %collective-permute-start.20 = (bf16[256,896]{0,1:T(8,128)(2,1)S(1)}, bf16[256,896]{0,1:T(8,128)(2,1)S(1)}, u32[]{:S(2)}, u32[]{:S(2)}) collective-permute-start(bf16[256,896]{0,1:T(8,128)(2,1)S(1)} %add_convert_fusion), channel_id=1, source_target_pairs={{0,8},{2,10},{4,12},{6,14},{8,0},{10,2},{12,4},{14,6},{17,25},{19,... | collective-permute-start | bytes 1376264 | tf_op jit(solution)/shard_map/ppermute | solution.py:148
  213.2 9.8 %collective-permute-done.20 = bf16[256,896]{0,1:T(8,128)(2,1)S(1)} collective-permute-done((bf16[256,896]{0,1:T(8,128)(2,1)S(1)}, bf16[256,896]{0,1:T(8,128)(2,1)S(1)}, u32[]{:S(2)}, u32[]{:S(2)}) %collective-permute-start.20) | collective-permute-done | bytes 458784 | tf_op jit(solution)/shard_map/ppermute | solution.py:148
  223.6 1.4 copy.22
  (85 shorter events, 10.0 us)
Async XLA Ops:
  1.9 15.8 %copy-start.8 = (s32[256]{0:T(256)S(1)}, s32[256]{0:T(256)}, u32[]{:S(2)}) copy-start(s32[256]{0:T(256)} %param.10) | copy-start | bytes 3076
  2.1 15.8 %collective-permute-start = (bf16[256,640]{1,0:T(8,128)(2,1)S(1)}, bf16[256,640]{1,0:T(8,128)(2,1)S(1)}, u32[]{:S(2)}, u32[]{:S(2)}) collective-permute-start(bf16[256,640]{1,0:T(8,128)(2,1)S(1)} %pad_maximum_fusion.12), channel_id=1, source_target_pairs={{0,8},{2,10},{4,12},{6,14},{8,16},{10,18},{12,20},{14,22},{16,24},... | collective-permute-start | bytes 983048 | tf_op jit(solution)/shard_map/ppermute | solution.py:26
  5.6 15.1 %collective-permute-start.1 = (bf16[256,640]{1,0:T(8,128)(2,1)S(1)}, bf16[256,640]{1,0:T(8,128)(2,1)S(1)}, u32[]{:S(2)}, u32[]{:S(2)}) collective-permute-start(bf16[256,640]{1,0:T(8,128)(2,1)S(1)} %pad_maximum_fusion.12), channel_id=1, source_target_pairs={{0,6},{2,8},{4,10},{6,12},{8,14},{10,16},{12,18},{14,20},{16,22},{... | collective-permute-start | bytes 983048 | tf_op jit(solution)/shard_map/ppermute | solution.py:26
  8.2 19.6 %collective-permute-start.2 = (bf16[256,640]{1,0:T(8,128)(2,1)S(1)}, bf16[256,640]{1,0:T(8,128)(2,1)S(1)}, u32[]{:S(2)}, u32[]{:S(2)}) collective-permute-start(bf16[256,640]{1,0:T(8,128)(2,1)S(1)} %pad_maximum_fusion.12), channel_id=1, source_target_pairs={{0,4},{2,6},{4,8},{6,10},{8,12},{10,14},{12,16},{14,18},{16,20},{1... | collective-permute-start | bytes 983048 | tf_op jit(solution)/shard_map/ppermute | solution.py:26
  11.6 16.4 %collective-permute-start.3 = (bf16[256,640]{1,0:T(8,128)(2,1)S(1)}, bf16[256,640]{1,0:T(8,128)(2,1)S(1)}, u32[]{:S(2)}, u32[]{:S(2)}) collective-permute-start(bf16[256,640]{1,0:T(8,128)(2,1)S(1)} %pad_maximum_fusion.12), channel_id=1, source_target_pairs={{0,2},{2,4},{4,6},{6,8},{8,10},{10,12},{12,14},{14,16},{16,18},{18... | collective-permute-start | bytes 983048 | tf_op jit(solution)/shard_map/ppermute | solution.py:26
  14.2 45.9 %collective-permute-start.4 = (bf16[224,4096]{1,0:T(8,128)(2,1)}, bf16[224,4096]{1,0:T(8,128)(2,1)}, u32[]{:S(2)}, u32[]{:S(2)}) collective-permute-start(bf16[224,4096]{1,0:T(8,128)(2,1)} %bitcast.50), channel_id=1, source_target_pairs={{0,4},{2,6},{4,0},{6,2},{8,12},{10,14},{12,8},{14,10},{16,20},{18,... | collective-permute-start | bytes 5505032 | tf_op jit(solution)/shard_map/ppermute | solution.py:120
  17.9 105.8 %collective-permute-start.11 = (bf16[112,4096]{1,0:T(8,128)(2,1)}, bf16[112,4096]{1,0:T(8,128)(2,1)}, u32[]{:S(2)}, u32[]{:S(2)}) collective-permute-start(bf16[112,4096]{1,0:T(8,128)(2,1)} %get-tuple-element.28), channel_id=1, source_target_pairs={{0,16},{2,18},{4,20},{6,22},{8,24},{10,26},{12,28},{14,30},{16,0},... | collective-permute-start | bytes 2752520 | tf_op jit(solution)/shard_map/ppermute | solution.py:120
  28.4 1.6 copy-start
  28.4 1.8 copy-start.1
  30.2 9.7 %copy-start.3 = (bf16[2,1280,128]{2,1,0:T(8,128)(2,1)}, bf16[2,1280,128]{2,1,0:T(8,128)(2,1)S(1)}, u32[]{:S(2)}) copy-start(bf16[2,1280,128]{2,1,0:T(8,128)(2,1)S(1)} %pad_maximum_fusion.5.tails) | copy-start | bytes 1966084
  40.0 0.9 copy-start.5
  40.8 94.3 %collective-permute-start.15 = (bf16[112,4096]{1,0:T(8,128)(2,1)}, bf16[112,4096]{1,0:T(8,128)(2,1)}, u32[]{:S(2)}, u32[]{:S(2)}) collective-permute-start(bf16[112,4096]{1,0:T(8,128)(2,1)} %get-tuple-element.22), channel_id=1, source_target_pairs={{0,16},{2,18},{4,20},{6,22},{8,24},{10,26},{12,28},{14,30},{16,0},... | collective-permute-start | bytes 2752520 | tf_op jit(solution)/shard_map/ppermute | solution.py:120
  43.4 56.3 %collective-permute-start.7 = (bf16[256,1024]{1,0:T(8,128)(2,1)}, bf16[256,1024]{1,0:T(8,128)(2,1)S(1)}, u32[]{:S(2)}, u32[]{:S(2)}) collective-permute-start(bf16[256,1024]{1,0:T(8,128)(2,1)} %copy-done.5), channel_id=1, source_target_pairs={{0,8},{2,10},{4,12},{6,14},{8,0},{10,2},{12,4},{14,6},{16,24},{18,... | collective-permute-start | bytes 1572872 | tf_op jit(solution)/shard_map/ppermute | solution.py:120
  43.4 1.2 copy-start.2
  44.7 1.1 copy-start.4
  45.8 14.4 %copy-start.7 = (bf16[4096,224]{0,1:T(8,128)(2,1)S(1)}, bf16[4096,224]{0,1:T(8,128)(2,1)}, u32[]{:S(2)}) copy-start(bf16[4096,224]{0,1:T(8,128)(2,1)} %param.13) | copy-start | bytes 5505028
  55.4 46.8 %collective-permute-start.8 = (bf16[256,1024]{1,0:T(8,128)(2,1)S(1)}, bf16[256,1024]{1,0:T(8,128)(2,1)S(1)}, u32[]{:S(2)}, u32[]{:S(2)}) collective-permute-start(bf16[256,1024]{1,0:T(8,128)(2,1)S(1)} %attention.5), channel_id=1, source_target_pairs={{0,8},{2,10},{4,12},{6,14},{8,0},{10,2},{12,4},{14,6},{16,24},{18,... | collective-permute-start | bytes 1572872 | tf_op jit(solution)/shard_map/ppermute | solution.py:120
  62.0 109.0 %collective-permute-start.5 = (bf16[448,4096]{1,0:T(8,128)(2,1)S(1)}, bf16[448,4096]{1,0:T(8,128)(2,1)}, u32[]{:S(2)}, u32[]{:S(2)}) collective-permute-start(bf16[448,4096]{1,0:T(8,128)(2,1)S(1)} %pad_maximum_fusion), channel_id=1, source_target_pairs={{0,2},{2,0},{4,6},{6,4},{8,10},{10,8},{12,14},{14,12},{16,18},{18,... | collective-permute-start | bytes 11010056 | tf_op jit(solution)/shard_map/ppermute | solution.py:120
  111.8 28.8 %collective-permute-start.9 = (bf16[256,1024]{1,0:T(8,128)(2,1)S(1)}, bf16[256,1024]{1,0:T(8,128)(2,1)S(1)}, u32[]{:S(2)}, u32[]{:S(2)}) collective-permute-start(bf16[256,1024]{1,0:T(8,128)(2,1)S(1)} %attention.6), channel_id=1, source_target_pairs={{0,8},{2,10},{4,12},{6,14},{8,0},{10,2},{12,4},{14,6},{16,24},{18,... | collective-permute-start | bytes 1572872 | tf_op jit(solution)/shard_map/ppermute | solution.py:120
  121.7 14.8 %copy-start.6 = (bf16[256,1024]{1,0:T(8,128)(2,1)S(1)}, bf16[256,1024]{1,0:T(8,128)(2,1)}, u32[]{:S(2)}) copy-start(bf16[256,1024]{1,0:T(8,128)(2,1)} %copy-done.5) | copy-start | bytes 1572868
  121.7 35.1 %collective-permute-start.10 = (bf16[256,1024]{1,0:T(8,128)(2,1)S(1)}, bf16[256,1024]{1,0:T(8,128)(2,1)S(1)}, u32[]{:S(2)}, u32[]{:S(2)}) collective-permute-start(bf16[256,1024]{1,0:T(8,128)(2,1)S(1)} %attention.7), channel_id=1, source_target_pairs={{0,8},{2,10},{4,12},{6,14},{8,0},{10,2},{12,4},{14,6},{16,24},{18,... | collective-permute-start | bytes 1572872 | tf_op jit(solution)/shard_map/ppermute | solution.py:120
  123.7 32.9 %collective-permute-start.12 = (bf16[112,4096]{1,0:T(8,128)(2,1)}, bf16[112,4096]{1,0:T(8,128)(2,1)S(1)}, u32[]{:S(2)}, u32[]{:S(2)}) collective-permute-start(bf16[112,4096]{1,0:T(8,128)(2,1)} %collective-permute-done.11), channel_id=1, source_target_pairs={{0,4},{2,6},{4,0},{6,2},{8,12},{10,14},{12,8},{14,10},{16,20},{18,... | collective-permute-start | bytes 2752520 | tf_op jit(solution)/shard_map/ppermute | solution.py:120
  135.2 35.7 %collective-permute-start.16 = (bf16[112,4096]{1,0:T(8,128)(2,1)}, bf16[112,4096]{1,0:T(8,128)(2,1)S(1)}, u32[]{:S(2)}, u32[]{:S(2)}) collective-permute-start(bf16[112,4096]{1,0:T(8,128)(2,1)} %collective-permute-done.15), channel_id=1, source_target_pairs={{0,4},{2,6},{4,0},{6,2},{8,12},{10,14},{12,8},{14,10},{16,20},{18,... | collective-permute-start | bytes 2752520 | tf_op jit(solution)/shard_map/ppermute | solution.py:120
  156.7 19.6 %collective-permute-start.13 = (bf16[224,4096]{1,0:T(8,128)(2,1)S(1)}, bf16[224,4096]{1,0:T(8,128)(2,1)S(1)}, u32[]{:S(2)}, u32[]{:S(2)}) collective-permute-start(bf16[224,4096]{1,0:T(8,128)(2,1)S(1)} %constant_dynamic-update-slice_fusion.5), channel_id=1, source_target_pairs={{0,2},{2,0},{4,6},{6,4},{8,10},{10,8},{12,14},{14,12},{16,18},{18,... | collective-permute-start | bytes 5505032 | tf_op jit(solution)/shard_map/ppermute | solution.py:120
  170.9 16.2 %collective-permute-start.17 = (bf16[224,4096]{1,0:T(8,128)(2,1)S(1)}, bf16[224,4096]{1,0:T(8,128)(2,1)S(1)}, u32[]{:S(2)}, u32[]{:S(2)}) collective-permute-start(bf16[224,4096]{1,0:T(8,128)(2,1)S(1)} %constant_dynamic-update-slice_fusion.7), channel_id=1, source_target_pairs={{0,2},{2,0},{4,6},{6,4},{8,10},{10,8},{12,14},{14,12},{16,18},{18,... | collective-permute-start | bytes 5505032 | tf_op jit(solution)/shard_map/ppermute | solution.py:120
  174.3 36.3 %collective-permute-start.19 = (bf16[256,896]{0,1:T(8,128)(2,1)S(1)}, bf16[256,896]{0,1:T(8,128)(2,1)S(1)}, u32[]{:S(2)}, u32[]{:S(2)}) collective-permute-start(bf16[256,896]{0,1:T(8,128)(2,1)S(1)} %fusion.7), channel_id=1, source_target_pairs={{1,0},{3,2},{5,4},{7,6},{9,8},{11,10},{13,12},{15,14},{16,17},{18,... | collective-permute-start | bytes 1376264 | tf_op jit(solution)/shard_map/ppermute | solution.py:143
  177.2 29.4 %collective-permute-start.21 = (bf16[256,448]{0,1:T(8,128)(2,1)S(1)}, bf16[256,448]{0,1:T(8,128)(2,1)S(1)}, u32[]{:S(2)}, u32[]{:S(2)}) collective-permute-start(bf16[256,448]{0,1:T(8,128)(2,1)S(1)} %fusion.6), channel_id=1, source_target_pairs={{0,1},{2,3},{4,5},{6,7},{8,9},{10,11},{12,13},{14,15},{17,16},{19,... | collective-permute-start | bytes 688136 | tf_op jit(solution)/shard_map/ppermute | solution.py:143
  185.0 28.1 %collective-permute-start.6 = (bf16[256,896]{0,1:T(8,128)(2,1)S(1)}, bf16[256,896]{0,1:T(8,128)(2,1)S(1)}, u32[]{:S(2)}, u32[]{:S(2)}) collective-permute-start(bf16[256,896]{0,1:T(8,128)(2,1)S(1)} %fusion.1), channel_id=1, source_target_pairs={{1,0},{3,2},{5,4},{7,6},{9,8},{11,10},{13,12},{15,14},{16,17},{18,... | collective-permute-start | bytes 1376264 | tf_op jit(solution)/shard_map/ppermute | solution.py:143
  188.0 19.4 %collective-permute-start.18 = (bf16[256,448]{0,1:T(8,128)(2,1)S(1)}, bf16[256,448]{0,1:T(8,128)(2,1)S(1)}, u32[]{:S(2)}, u32[]{:S(2)}) collective-permute-start(bf16[256,448]{0,1:T(8,128)(2,1)S(1)} %fusion.3), channel_id=1, source_target_pairs={{0,1},{2,3},{4,5},{6,7},{8,9},{10,11},{12,13},{14,15},{17,16},{19,... | collective-permute-start | bytes 688136 | tf_op jit(solution)/shard_map/ppermute | solution.py:143
  195.0 7.1 %collective-permute-start.23 = (bf16[256,448]{0,1:T(8,128)(2,1)S(1)}, bf16[256,448]{0,1:T(8,128)(2,1)S(1)}, u32[]{:S(2)}, u32[]{:S(2)}) collective-permute-start(bf16[256,448]{0,1:T(8,128)(2,1)S(1)} %fusion.2), channel_id=1, source_target_pairs={{0,1},{2,3},{4,5},{6,7},{8,9},{10,11},{12,13},{14,15},{17,16},{19,... | collective-permute-start | bytes 688136 | tf_op jit(solution)/shard_map/ppermute | solution.py:143
  202.1 8.4 %collective-permute-start.14 = (bf16[256,448]{0,1:T(8,128)(2,1)S(1)}, bf16[256,448]{0,1:T(8,128)(2,1)S(1)}, u32[]{:S(2)}, u32[]{:S(2)}) collective-permute-start(bf16[256,448]{0,1:T(8,128)(2,1)S(1)} %fusion.4), channel_id=1, source_target_pairs={{0,1},{2,3},{4,5},{6,7},{8,9},{10,11},{12,13},{14,15},{17,16},{19,... | collective-permute-start | bytes 688136 | tf_op jit(solution)/shard_map/ppermute | solution.py:143
  206.6 6.4 %collective-permute-start.24 = (bf16[256,448]{0,1:T(8,128)(2,1)S(1)}, bf16[256,448]{0,1:T(8,128)(2,1)S(1)}, u32[]{:S(2)}, u32[]{:S(2)}) collective-permute-start(bf16[256,448]{0,1:T(8,128)(2,1)S(1)} %add_convert_fusion.2), channel_id=1, source_target_pairs={{1,9},{3,11},{5,13},{7,15},{9,1},{11,3},{13,5},{15,7},{16,24},{18,... | collective-permute-start | bytes 688136 | tf_op jit(solution)/shard_map/ppermute | solution.py:148
  207.3 5.7 %collective-permute-start.22 = (bf16[256,448]{0,1:T(8,128)(2,1)S(1)}, bf16[256,448]{0,1:T(8,128)(2,1)S(1)}, u32[]{:S(2)}, u32[]{:S(2)}) collective-permute-start(bf16[256,448]{0,1:T(8,128)(2,1)S(1)} %add_convert_fusion.3), channel_id=1, source_target_pairs={{1,9},{3,11},{5,13},{7,15},{9,1},{11,3},{13,5},{15,7},{16,24},{18,... | collective-permute-start | bytes 688136 | tf_op jit(solution)/shard_map/ppermute | solution.py:148
  210.7 12.4 %collective-permute-start.20 = (bf16[256,896]{0,1:T(8,128)(2,1)S(1)}, bf16[256,896]{0,1:T(8,128)(2,1)S(1)}, u32[]{:S(2)}, u32[]{:S(2)}) collective-permute-start(bf16[256,896]{0,1:T(8,128)(2,1)S(1)} %add_convert_fusion), channel_id=1, source_target_pairs={{0,8},{2,10},{4,12},{6,14},{8,0},{10,2},{12,4},{14,6},{17,25},{19,... | collective-permute-start | bytes 1376264 | tf_op jit(solution)/shard_map/ppermute | solution.py:148

commit v4 on v1

--- a/solution.py
+++ b/solution.py
@@ -15,7 +15,9 @@
 HOPS = 4
 MARKS = 64
 FAR = 1e30
-PIECES = 2
+PLANE = 4
+PARTS = 2
+COST = 1 << 20
 
 
 def from_behind(value, steps):
@@ -49,47 +51,37 @@
         out[:, cols] = (total[:, :VD] / total[:, VD:]).astype(jnp.bfloat16)
 
 
-def attention(q_nope, q_rope, q_mark, content, tails, w_uk, w_uv):
-    rows, width = q_nope.shape
+def attention(start, pairs, q_nope, q_rope, q_mark, content, tails, w_uk, w_uv):
+    rows = q_nope.shape[0]
+    width = 2 * HD * pairs
     keys = content.shape[0]
-    pairs = width // (2 * HD)
     whole = lambda *shape: pl.BlockSpec(shape, lambda i: (0,) * len(shape))
     return pl.pallas_call(
         functools.partial(attend, rows),
         out_shape=jax.ShapeDtypeStruct((rows, width), jnp.bfloat16),
         grid=(pairs,),
         in_specs=[
-            pl.BlockSpec((rows, 2 * HD), lambda i: (0, i)),
-            pl.BlockSpec((rows, 2 * ROPE), lambda i: (0, i)),
+            pl.BlockSpec((rows, 2 * HD), lambda i: (0, i + start)),
+            pl.BlockSpec((rows, 2 * ROPE), lambda i: (0, i + start)),
             whole(rows, 2 * ROPE),
             whole(keys, LAT),
             whole(2, keys, 2 * ROPE),
-            pl.BlockSpec((LAT, 2 * HD), lambda i: (0, i)),
-            pl.BlockSpec((LAT, 2 * HD), lambda i: (0, i)),
+            pl.BlockSpec((LAT, 2 * HD), lambda i: (0, i + start)),
+            pl.BlockSpec((LAT, 2 * HD), lambda i: (0, i + start)),
         ],
         out_specs=pl.BlockSpec((rows, 2 * VD), lambda i: (0, i)),
         compiler_params=pltpu.CompilerParams(
             dimension_semantics=("arbitrary",), vmem_limit_bytes=48 << 20
         ),
-        cost_estimate=pl.CostEstimate(
-            flops=pairs * 2 * keys * (2 * LAT * 2 * HD + 4 * rows * 2 * HD),
-            bytes_accessed=2 * (rows * width * 3 + LAT * width * 2),
-            transcendentals=pairs * 2 * rows * keys,
-        ),
+        cost_estimate=pl.CostEstimate(flops=COST, bytes_accessed=COST, transcendentals=0),
         name="attention",
     )(q_nope, q_rope, q_mark, content, tails, w_uk, w_uv)
 
 
 def shards(q_nope, q_rope, latent, doc_ids, w_uk, w_uv, w_out):
-    rows = q_nope.shape[0]
-    count = lax.axis_size("seq")
+    count, heads = lax.axis_size("seq"), lax.axis_size("head")
     position = lax.axis_index("seq")
     w_rows = w_out.T
-    step = w_rows.shape[0] // PIECES
-    gathered = [
-        lax.all_gather(w_rows[i * step : (i + 1) * step], "seq", axis=0, tiled=True)
-        for i in range(PIECES)
-    ]
     marks = (doc_ids[:, None] == jnp.arange(MARKS, dtype=jnp.int32)[None, :]).astype(jnp.bfloat16)
     payload = jnp.concatenate([latent, marks], axis=1)
     blocks = []
@@ -110,18 +102,25 @@
     )
     q_mark = (marks - jnp.bfloat16(1)) * jnp.bfloat16(FAR)
     q_mark = jnp.concatenate([q_mark, q_mark], axis=1)
-    attended = attention(q_nope, q_rope, q_mark, content, tails, w_uk, w_uv)
-    heads = lax.axis_size("head")
-    mine = lax.axis_index("head")
-    swap = [(a, b) for a in range(heads) for b in range(heads) if a != b]
-    parts = []
-    for piece in gathered:
-        share = lax.dot_general(
-            attended, piece, (((1,), (1,)), ((), ())), preferred_element_type=jnp.float32
-        )
-        parts.append(lax.psum_scatter(share, "head", scatter_dimension=1, tiled=True) if heads > 2 else exchange(share, mine))
-    joined = jnp.stack([part.reshape(rows, count // heads, step) for part in parts], axis=2)
-    return joined.reshape(rows, -1).astype(jnp.bfloat16)
+    fixed = (q_mark, content, tails)
+    if count == 4 * PLANE and heads == 2:
+        return paired(w_rows, q_nope, q_rope, fixed, w_uk, w_uv)
+    attended = attention(0, q_nope.shape[1] // (2 * HD), q_nope, q_rope, *fixed, w_uk, w_uv)
+    whole = lax.all_gather(w_rows, "seq", axis=0, tiled=True)
+    share = product(attended, whole)
+    return lax.psum_scatter(share, "head", scatter_dimension=1, tiled=True).astype(jnp.bfloat16)
+
+
+def product(left, right):
+    return lax.dot_general(left, right, (((1,), (1,)), ((), ())), preferred_element_type=jnp.float32)
+
+
+def swapped(value, bit):
+    return lax.ppermute(value, "seq", [(i, i ^ bit) for i in range(lax.axis_size("seq"))])
+
+
+def after(value, *earlier):
+    return lax.optimization_barrier((value, *earlier))[0]
 
 
 def exchange(share, mine):
@@ -129,7 +128,30 @@
     first, second = share[:, :half], share[:, half:]
     keep = jnp.where(mine == 0, first, second)
     give = jnp.where(mine == 0, second, first).astype(jnp.bfloat16)
-    return keep + lax.ppermute(give, "head", [(0, 1), (1, 0)]).astype(jnp.float32)
+    taken = lax.ppermute(give, "head", [(0, 1), (1, 0)])
+    return (keep + taken.astype(jnp.float32)).astype(jnp.bfloat16)
+
+
+def paired(w_rows, q_nope, q_rope, fixed, w_uk, w_uv):
+    width = q_nope.shape[1]
+    mine = lax.axis_index("head")
+    plane = lax.axis_index("seq") // PLANE
+    groups = [
+        [seq for seq in range(4 * PLANE) if seq // PLANE % 2 == parity] for parity in range(2)
+    ]
+    w_rows = after(w_rows, fixed[1])
+    columns = lax.all_gather(w_rows, "seq", axis=0, tiled=True, axis_index_groups=groups)
+    each = width // (2 * HD) // PARTS
+    own, partner = [], []
+    for i in range(PARTS):
+        mark = after(fixed[0], own[-1]) if own else fixed[0]
+        own.append(attention(i * each, each, q_nope, q_rope, mark, *fixed[1:], w_uk, w_uv))
+        partner.append(swapped(own[i], PLANE))
+    own, partner = jnp.concatenate(own, axis=1), jnp.concatenate(partner, axis=1)
+    here = exchange(product(own, columns), mine)
+    back = swapped(exchange(product(partner, columns), mine), PLANE)
+    even = plane % 2 == 0
+    return jnp.concatenate([jnp.where(even, here, back), jnp.where(even, back, here)], axis=1)
 
 
 def solution(mesh):

time: 290 us -> 234 us (0.81)
  waiting for transfers between devices: 194 us -> 128 us
  other arithmetic: 4.14 us -> 10.9 us
  starting transfers between devices: 15.3 us -> 21 us
  local copies, waits for them, and re-layouts: 8.72 us -> 4.6 us
    all_gather x2 -> x1, waiting for transfers between devices: 155 us -> 17.5 us  [paired(): lax.all_gather(w_rows, 'seq', axis=0, tiled=True, axis_index_groups=groups)]
    ppermute x2 -> x5, waiting for transfers between devices: 9.92 us -> 98.2 us  [the longest x3 88.9 us: swapped(): lax.ppermute(value, 'seq', [(i, i ^ bit) for i in range(lax.axis_size('se...]
    ppermute x4, waiting for transfers between devices: 28.8 us -> 11.8 us  [from_behind(): lax.ppermute(value, 'seq', [(source, source + steps) for source in range(...]
    ppermute x2 -> x5, starting transfers between devices: 3.07 us -> 7.08 us  [the longest x3 4.99 us: swapped(): lax.ppermute(value, 'seq', [(i, i ^ bit) for i in range(lax.axis_size('se...]
    slice x1 -> x0, local copies, waits for them, and re-layouts: 2.96 us -> none  [shards(): w_rows[i * step:(i + 1) * step]]
    pallas_call x1 -> x2, Pallas kernels: 34.9 us -> 36.2 us  [attention(): pl.pallas_call(functools.partial(attend, rows), out_shape=jax.ShapeDtypeS...]
  transfers between devices with their start and end apart: 8 -> 10, of which waited for: 6 -> 7; matrix products, arithmetic and copies ran while one was open for 7% -> 6% of each run, Pallas kernels for 12% -> 16%
where the time goes in v4:
time: 234 us; the launch traced here: 232 us
  waiting for transfers between devices  128 us (55%)
  Pallas kernels  36.2 us (15%)
  starting transfers between devices  21 us (9%)
  matrix products  18.6 us (8%)
  between operations  13.6 us (6%)
  other arithmetic  10.9 us (5%)
  local copies, waits for them, and re-layouts  4.6 us (2%)
    ppermute x3, waiting for transfers between devices, swapped(): lax.ppermute(value, 'seq', [(i, i ^ bit) for i in range(lax.axis_size('se...  88.9 us
    pallas_call x2, Pallas kernels, attention(): pl.pallas_call(functools.partial(attend, rows), out_shape=jax.ShapeDtypeS...  36.2 us
    dot_general x2, matrix products, product(): lax.dot_general(left, right, (((1,), (1,)), ((), ())), preferred_element_...  18.6 us
    all_gather x1, waiting for transfers between devices, paired(): lax.all_gather(w_rows, 'seq', axis=0, tiled=True, axis_index_groups=groups)  17.5 us
    ppermute x4, starting transfers between devices, from_behind(): lax.ppermute(value, 'seq', [(source, source + steps) for source in range(...  13.9 us
    ppermute x4, waiting for transfers between devices, from_behind(): lax.ppermute(value, 'seq', [(source, source + steps) for source in range(...  11.8 us
    ppermute x2, waiting for transfers between devices, exchange(): taken = lax.ppermute(give, 'head', [(0, 1), (1, 0)])  9.35 us
    ppermute x3, starting transfers between devices, swapped(): lax.ppermute(value, 'seq', [(i, i ^ bit) for i in range(lax.axis_size('se...  4.99 us
  transfers between devices with their start and end apart: 10, of which 7 were waited for; matrix products, arithmetic and copies ran while one was open for 6% of the time, Pallas kernels for 16%

profile of v4, /device:TPU:4, one launch (start us, length us, event | category | flops | bytes accessed | tf_op | source)
XLA Modules:
  0.0 232.3 jit_solution(10081469482323406226)
XLA Ops:
  6.5 0.8 fusion.8
  7.3 1.2 copy.8
  8.5 0.8 pad_maximum_fusion.2
  9.3 3.5 %collective-permute-start = (bf16[256,640]{1,0:T(8,128)(2,1)}, bf16[256,640]{1,0:T(8,128)(2,1)S(1)}, u32[]{:S(2)}, u32[]{:S(2)}) collective-permute-start(bf16[256,640]{1,0:T(8,128)(2,1)} %pad_maximum_fusion.2), channel_id=1, source_target_pairs={{0,8},{2,10},{4,12},{6,14},{8,16},{10,18},{12,20},{14,22},{16,24},... | collective-permute-start | bytes 983048 | tf_op jit(solution)/shard_map/ppermute | solution.py:25
  12.8 1.9 collective-permute-start.3
  14.7 3.4 %collective-permute-start.2 = (bf16[256,640]{1,0:T(8,128)(2,1)}, bf16[256,640]{1,0:T(8,128)(2,1)S(1)}, u32[]{:S(2)}, u32[]{:S(2)}) collective-permute-start(bf16[256,640]{1,0:T(8,128)(2,1)} %pad_maximum_fusion.2), channel_id=1, source_target_pairs={{0,4},{2,6},{4,8},{6,10},{8,12},{10,14},{12,16},{14,18},{16,20},{1... | collective-permute-start | bytes 983048 | tf_op jit(solution)/shard_map/ppermute | solution.py:25
  18.1 5.1 %collective-permute-start.1 = (bf16[256,640]{1,0:T(8,128)(2,1)}, bf16[256,640]{1,0:T(8,128)(2,1)}, u32[]{:S(2)}, u32[]{:S(2)}) collective-permute-start(bf16[256,640]{1,0:T(8,128)(2,1)} %pad_maximum_fusion.2), channel_id=1, source_target_pairs={{0,6},{2,8},{4,10},{6,12},{8,14},{10,16},{12,18},{14,20},{16,22},{... | collective-permute-start | bytes 983048 | tf_op jit(solution)/shard_map/ppermute | solution.py:25
  23.3 0.1 slice_select_fusion.3
  23.4 0.1 maximum_dynamic-update-slice_fusion.3
  23.5 11.8 %collective-permute-done.1 = bf16[256,640]{1,0:T(8,128)(2,1)} collective-permute-done((bf16[256,640]{1,0:T(8,128)(2,1)}, bf16[256,640]{1,0:T(8,128)(2,1)}, u32[]{:S(2)}, u32[]{:S(2)}) %collective-permute-start.1) | collective-permute-done | bytes 327712 | tf_op jit(solution)/shard_map/ppermute | solution.py:25
  35.2 0.9 slice_select_fusion.2
  36.2 1.1 maximum_dynamic-update-slice_fusion.2
  37.3 0.1 slice_select_fusion.1
  37.4 0.1 maximum_dynamic-update-slice_fusion.1
  37.5 0.1 slice_select_fusion
  37.6 0.1 maximum_dynamic-update-slice_fusion
  37.7 0.1 constant_dynamic-update-slice_fusion
  37.8 0.1 slice.69.content
  37.9 0.0 all-gather.2.cloned.1.call-update
  37.9 0.5 copy-done.4
  38.5 0.1 add_multiply_fusion
  38.6 0.1 pad_maximum_fusion.3.q_mark
  38.7 0.2 fusion.11
  38.9 0.2 slice_bitcast_fusion
  39.1 0.1 pad_maximum_fusion.1.tails
  39.2 1.1 copy-done
  40.3 0.3 copy-done.1
  40.5 18.1 %attention.2 = bf16[256,2048]{1,0:T(8,128)(2,1)S(1)} custom-call(bf16[256,4096]{1,0:T(8,128)(2,1)S(1)} %copy-done, bf16[256,2048]{1,0:T(8,128)(2,1)S(1)} %copy-done.1, bf16[256,128]{1,0:T(8,128)(2,1)S(1)} %pad_maximum_fusion.3.q_mark, bf16[1280,512]{1,0:T(8,128)(2,1)S(1)} %slice.69.content, bf16[2,1280,128]{2,1,0:T(8,128)(2,1)S(1)} %pad_maximum_fusion.1.tails, ...), custom_call_target="tpu_custom_call" | custom-call | flops 1048576 | bytes 1048576 | tf_op jit(solution)/shard_map/attention/pallas_call | solution.py:59
  58.6 18.1 %attention.3 = bf16[256,2048]{1,0:T(8,128)(2,1)S(1)} custom-call(bf16[256,4096]{1,0:T(8,128)(2,1)S(1)} %copy-done, bf16[256,2048]{1,0:T(8,128)(2,1)S(1)} %copy-done.1, bf16[256,128]{1,0:T(8,128)(2,1)S(1)} %pad_maximum_fusion.3.q_mark, bf16[1280,512]{1,0:T(8,128)(2,1)S(1)} %slice.69.content, bf16[2,1280,128]{2,1,0:T(8,128)(2,1)S(1)} %pad_maximum_fusion.1.tails, ...), custom_call_target="tpu_custom_call" | custom-call | flops 1048576 | bytes 1048576 | tf_op jit(solution)/shard_map/attention/pallas_call | solution.py:59
  76.7 4.9 %collective-permute-start.6 = (bf16[256,2048]{1,0:T(8,128)(2,1)S(1)}, bf16[256,2048]{1,0:T(8,128)(2,1)S(1)}, u32[]{:S(2)}, u32[]{:S(2)}) collective-permute-start(bf16[256,2048]{1,0:T(8,128)(2,1)S(1)} %attention.3), channel_id=1, source_target_pairs={{0,8},{2,10},{4,12},{6,14},{8,0},{10,2},{12,4},{14,6},{16,24},{18,... | collective-permute-start | bytes 3145736 | tf_op jit(solution)/shard_map/ppermute | solution.py:119
  81.6 0.1 collective-permute-start.5
  81.7 51.5 %collective-permute-done.6 = bf16[256,2048]{1,0:T(8,128)(2,1)S(1)} collective-permute-done((bf16[256,2048]{1,0:T(8,128)(2,1)S(1)}, bf16[256,2048]{1,0:T(8,128)(2,1)S(1)}, u32[]{:S(2)}, u32[]{:S(2)}) %collective-permute-start.6) | collective-permute-done | bytes 1048608 | tf_op jit(solution)/shard_map/ppermute | solution.py:119
  133.2 32.9 %collective-permute-done.5 = bf16[256,2048]{1,0:T(8,128)(2,1)} collective-permute-done((bf16[256,2048]{1,0:T(8,128)(2,1)S(1)}, bf16[256,2048]{1,0:T(8,128)(2,1)}, u32[]{:S(2)}, u32[]{:S(2)}) %collective-permute-start.5) | collective-permute-done | bytes 1048608 | tf_op jit(solution)/shard_map/ppermute | solution.py:119
  166.2 17.5 %all-gather.2.cloned.1.call-done = bf16[1792,4096]{1,0:T(8,128)(2,1)} async-done(((bf16[224,4096]{1,0:T(8,128)(2,1)}), bf16[1792,4096]{1,0:T(8,128)(2,1)}) %all-gather.2.cloned.1.call-update) | async-done | bytes 14680080 | tf_op jit(solution)/shard_map/all_gather | solution.py:143
  183.6 10.7 %fusion.4 = f32[256,1792]{1,0:T(8,128)} fusion(bf16[1792,4096]{1,0:T(8,128)(2,1)} %all-gather.2.cloned.1.call-done, bf16[256,2048]{1,0:T(8,128)(2,1)S(1)} %collective-permute-done.6, bf16[256,2048]{1,0:T(8,128)(2,1)} %collective-permute-done.5), kind=kOutput, calls=%fused_computation.4 | convolution fusion | flops 3762290688 | bytes 18612224 | tf_op jit(solution)/shard_map/dot_general | solution.py:115
  194.4 2.3 select_convert_fusion
  196.7 1.5 collective-permute-start.7
  198.1 7.8 %fusion = f32[256,1792]{1,0:T(8,128)S(1)} fusion(bf16[1792,4096]{1,0:T(8,128)(2,1)} %all-gather.2.cloned.1.call-done, bf16[256,2048]{1,0:T(8,128)(2,1)S(1)} %attention.3, bf16[256,2048]{1,0:T(8,128)(2,1)S(1)} %attention.2), kind=kOutput, calls=%fused_computation | convolution fusion | flops 3762290688 | bytes 18612224 | tf_op jit(solution)/shard_map/dot_general | solution.py:115
  206.0 1.2 copy-done.2
  207.2 0.1 select_convert_fusion.1
  207.3 0.6 collective-permute-start.4
  208.0 1.7 collective-permute-done.7
  209.7 2.5 %add_convert_fusion = bf16[256,896]{1,0:T(8,128)(2,1)} fusion(bf16[256,896]{1,0:T(8,128)(2,1)} %collective-permute-done.7, f32[256,1792]{1,0:T(8,128)} %fusion.4, pred[]{:T(512)S(6)} %eq.13), kind=kLoop, calls=%fused_computation.9 | loop fusion | flops 917504 | bytes 2752513 | tf_op jit(solution)/shard_map/convert_element_type | solution.py:132
  212.2 7.6 %collective-permute-done.4 = bf16[256,896]{1,0:T(8,128)(2,1)S(1)} collective-permute-done((bf16[256,896]{1,0:T(8,128)(2,1)S(1)}, bf16[256,896]{1,0:T(8,128)(2,1)S(1)}, u32[]{:S(2)}, u32[]{:S(2)}) %collective-permute-start.4) | collective-permute-done | bytes 458784 | tf_op jit(solution)/shard_map/ppermute | solution.py:131
  219.8 4.4 %collective-permute-done.8 = bf16[256,896]{1,0:T(8,128)(2,1)S(1)} collective-permute-done((bf16[256,896]{1,0:T(8,128)(2,1)}, bf16[256,896]{1,0:T(8,128)(2,1)S(1)}, u32[]{:S(2)}, u32[]{:S(2)}) %collective-permute-start.8) | collective-permute-done | bytes 458784 | tf_op jit(solution)/shard_map/ppermute | solution.py:119
  224.3 0.2 broadcast_select_fusion.1
  224.4 0.1 broadcast_select_fusion
  224.5 1.0 pad_maximum_fusion
  (11 shorter events, 0.0 us)
Async XLA Ops:
  6.5 177.1 %all-gather.2.cloned.1.call-start = ((), (), s32[]{:S(2)}) async-start(), calls=%async_computation | async-start | bytes 16515072 | tf_op jit(solution)/shard_map/all_gather | solution.py:143
  9.3 14.0 %collective-permute-start = (bf16[256,640]{1,0:T(8,128)(2,1)}, bf16[256,640]{1,0:T(8,128)(2,1)S(1)}, u32[]{:S(2)}, u32[]{:S(2)}) collective-permute-start(bf16[256,640]{1,0:T(8,128)(2,1)} %pad_maximum_fusion.2), channel_id=1, source_target_pairs={{0,8},{2,10},{4,12},{6,14},{8,16},{10,18},{12,20},{14,22},{16,24},... | collective-permute-start | bytes 983048 | tf_op jit(solution)/shard_map/ppermute | solution.py:25
  12.8 24.7 %collective-permute-start.3 = (bf16[256,640]{1,0:T(8,128)(2,1)}, bf16[256,640]{1,0:T(8,128)(2,1)S(1)}, u32[]{:S(2)}, u32[]{:S(2)}) collective-permute-start(bf16[256,640]{1,0:T(8,128)(2,1)} %pad_maximum_fusion.2), channel_id=1, source_target_pairs={{0,2},{2,4},{4,6},{6,8},{8,10},{10,12},{12,14},{14,16},{16,18},{18... | collective-permute-start | bytes 983048 | tf_op jit(solution)/shard_map/ppermute | solution.py:25
  14.7 22.5 %collective-permute-start.2 = (bf16[256,640]{1,0:T(8,128)(2,1)}, bf16[256,640]{1,0:T(8,128)(2,1)S(1)}, u32[]{:S(2)}, u32[]{:S(2)}) collective-permute-start(bf16[256,640]{1,0:T(8,128)(2,1)} %pad_maximum_fusion.2), channel_id=1, source_target_pairs={{0,4},{2,6},{4,8},{6,10},{8,12},{10,14},{12,16},{14,18},{16,20},{1... | collective-permute-start | bytes 983048 | tf_op jit(solution)/shard_map/ppermute | solution.py:25
  18.1 17.1 %collective-permute-start.1 = (bf16[256,640]{1,0:T(8,128)(2,1)}, bf16[256,640]{1,0:T(8,128)(2,1)}, u32[]{:S(2)}, u32[]{:S(2)}) collective-permute-start(bf16[256,640]{1,0:T(8,128)(2,1)} %pad_maximum_fusion.2), channel_id=1, source_target_pairs={{0,6},{2,8},{4,10},{6,12},{8,14},{10,16},{12,18},{14,20},{16,22},{... | collective-permute-start | bytes 983048 | tf_op jit(solution)/shard_map/ppermute | solution.py:25
  37.8 0.7 copy-start.4
  38.7 1.6 copy-start
  38.7 1.8 copy-start.1
  76.7 56.5 %collective-permute-start.6 = (bf16[256,2048]{1,0:T(8,128)(2,1)S(1)}, bf16[256,2048]{1,0:T(8,128)(2,1)S(1)}, u32[]{:S(2)}, u32[]{:S(2)}) collective-permute-start(bf16[256,2048]{1,0:T(8,128)(2,1)S(1)} %attention.3), channel_id=1, source_target_pairs={{0,8},{2,10},{4,12},{6,14},{8,0},{10,2},{12,4},{14,6},{16,24},{18,... | collective-permute-start | bytes 3145736 | tf_op jit(solution)/shard_map/ppermute | solution.py:119
  81.6 84.5 %collective-permute-start.5 = (bf16[256,2048]{1,0:T(8,128)(2,1)S(1)}, bf16[256,2048]{1,0:T(8,128)(2,1)}, u32[]{:S(2)}, u32[]{:S(2)}) collective-permute-start(bf16[256,2048]{1,0:T(8,128)(2,1)S(1)} %attention.2), channel_id=1, source_target_pairs={{0,8},{2,10},{4,12},{6,14},{8,0},{10,2},{12,4},{14,6},{16,24},{18,... | collective-permute-start | bytes 3145736 | tf_op jit(solution)/shard_map/ppermute | solution.py:119
  196.7 13.0 %collective-permute-start.7 = (bf16[256,896]{1,0:T(8,128)(2,1)}, bf16[256,896]{1,0:T(8,128)(2,1)}, u32[]{:S(2)}, u32[]{:S(2)}) collective-permute-start(bf16[256,896]{1,0:T(8,128)(2,1)} %select_convert_fusion), channel_id=1, source_target_pairs={{0,1},{1,0},{2,3},{3,2},{4,5},{5,4},{6,7},{7,6},{8,9},{9,8},{10,11... | collective-permute-start | bytes 1376264 | tf_op jit(solution)/shard_map/ppermute | solution.py:131
  206.0 1.3 copy-start.2
  207.3 16.9 %copy-start.3 = (f32[256,1792]{1,0:T(8,128)S(1)}, f32[256,1792]{1,0:T(8,128)}, u32[]{:S(2)}) copy-start(f32[256,1792]{1,0:T(8,128)} %copy-done.2) | copy-start | bytes 5505028
  207.3 12.5 %collective-permute-start.4 = (bf16[256,896]{1,0:T(8,128)(2,1)S(1)}, bf16[256,896]{1,0:T(8,128)(2,1)S(1)}, u32[]{:S(2)}, u32[]{:S(2)}) collective-permute-start(bf16[256,896]{1,0:T(8,128)(2,1)S(1)} %select_convert_fusion.1), channel_id=1, source_target_pairs={{0,1},{1,0},{2,3},{3,2},{4,5},{5,4},{6,7},{7,6},{8,9},{9,8},{10,11... | collective-permute-start | bytes 1376264 | tf_op jit(solution)/shard_map/ppermute | solution.py:131
  212.2 12.1 %collective-permute-start.8 = (bf16[256,896]{1,0:T(8,128)(2,1)}, bf16[256,896]{1,0:T(8,128)(2,1)S(1)}, u32[]{:S(2)}, u32[]{:S(2)}) collective-permute-start(bf16[256,896]{1,0:T(8,128)(2,1)} %add_convert_fusion), channel_id=1, source_target_pairs={{0,8},{2,10},{4,12},{6,14},{8,0},{10,2},{12,4},{14,6},{16,24},{18,... | collective-permute-start | bytes 1376264 | tf_op jit(solution)/shard_map/ppermute | solution.py:119
Sparse Core Ops, SparseCore 0:
  38.1 145.5 all-gather.1

commit v5 on v4

--- a/solution.py
+++ b/solution.py
@@ -15,8 +15,6 @@
 HOPS = 4
 MARKS = 64
 FAR = 1e30
-PLANE = 4
-PARTS = 2
 COST = 1 << 20
 
 
@@ -79,9 +77,9 @@
 
 
 def shards(q_nope, q_rope, latent, doc_ids, w_uk, w_uv, w_out):
-    count, heads = lax.axis_size("seq"), lax.axis_size("head")
+    heads = lax.axis_size("head")
     position = lax.axis_index("seq")
-    w_rows = w_out.T
+    whole = lax.all_gather(w_out, "seq", axis=1, tiled=True)
     marks = (doc_ids[:, None] == jnp.arange(MARKS, dtype=jnp.int32)[None, :]).astype(jnp.bfloat16)
     payload = jnp.concatenate([latent, marks], axis=1)
     blocks = []
@@ -103,24 +101,11 @@
     q_mark = (marks - jnp.bfloat16(1)) * jnp.bfloat16(FAR)
     q_mark = jnp.concatenate([q_mark, q_mark], axis=1)
     fixed = (q_mark, content, tails)
-    if count == 4 * PLANE and heads == 2:
-        return paired(w_rows, q_nope, q_rope, fixed, w_uk, w_uv)
     attended = attention(0, q_nope.shape[1] // (2 * HD), q_nope, q_rope, *fixed, w_uk, w_uv)
-    whole = lax.all_gather(w_rows, "seq", axis=0, tiled=True)
-    share = product(attended, whole)
+    share = jnp.dot(attended, whole, preferred_element_type=jnp.float32)
+    if heads == 2:
+        return exchange(share, lax.axis_index("head"))
     return lax.psum_scatter(share, "head", scatter_dimension=1, tiled=True).astype(jnp.bfloat16)
-
-
-def product(left, right):
-    return lax.dot_general(left, right, (((1,), (1,)), ((), ())), preferred_element_type=jnp.float32)
-
-
-def swapped(value, bit):
-    return lax.ppermute(value, "seq", [(i, i ^ bit) for i in range(lax.axis_size("seq"))])
-
-
-def after(value, *earlier):
-    return lax.optimization_barrier((value, *earlier))[0]
 
 
 def exchange(share, mine):
@@ -130,28 +115,6 @@
     give = jnp.where(mine == 0, second, first).astype(jnp.bfloat16)
     taken = lax.ppermute(give, "head", [(0, 1), (1, 0)])
     return (keep + taken.astype(jnp.float32)).astype(jnp.bfloat16)
-
-
-def paired(w_rows, q_nope, q_rope, fixed, w_uk, w_uv):
-    width = q_nope.shape[1]
-    mine = lax.axis_index("head")
-    plane = lax.axis_index("seq") // PLANE
-    groups = [
-        [seq for seq in range(4 * PLANE) if seq // PLANE % 2 == parity] for parity in range(2)
-    ]
-    w_rows = after(w_rows, fixed[1])
-    columns = lax.all_gather(w_rows, "seq", axis=0, tiled=True, axis_index_groups=groups)
-    each = width // (2 * HD) // PARTS
-    own, partner = [], []
-    for i in range(PARTS):
-        mark = after(fixed[0], own[-1]) if own else fixed[0]
-        own.append(attention(i * each, each, q_nope, q_rope, mark, *fixed[1:], w_uk, w_uv))
-        partner.append(swapped(own[i], PLANE))
-    own, partner = jnp.concatenate(own, axis=1), jnp.concatenate(partner, axis=1)
-    here = exchange(product(own, columns), mine)
-    back = swapped(exchange(product(partner, columns), mine), PLANE)
-    even = plane % 2 == 0
-    return jnp.concatenate([jnp.where(even, here, back), jnp.where(even, back, here)], axis=1)
 
 
 def solution(mesh):

time: 234 us -> 222 us (0.949)
  waiting for transfers between devices: 128 us -> 137 us
  other arithmetic: 10.9 us -> 2.97 us
  starting transfers between devices: 21 us -> 14.8 us
  matrix products: 18.6 us -> 13.6 us
  local copies, waits for them, and re-layouts: 4.6 us -> 1.46 us
    ppermute x3 -> x0, waiting for transfers between devices: 88.9 us -> none  [swapped(): lax.ppermute(value, 'seq', [(i, i ^ bit) for i in range(lax.axis_size('se...]
    all_gather x1, waiting for transfers between devices: 17.5 us -> 83 us  [shards(): whole = lax.all_gather(w_out, 'seq', axis=1, tiled=True)]
    ppermute x4, waiting for transfers between devices: 11.8 us -> 32.6 us  [from_behind(): lax.ppermute(value, 'seq', [(source, source + steps) for source in range(...]
    ppermute x2 -> x1, waiting for transfers between devices: 9.35 us -> 20.8 us  [exchange(): taken = lax.ppermute(give, 'head', [(0, 1), (1, 0)])]
    ppermute x3 -> x0, starting transfers between devices: 4.99 us -> none  [swapped(): lax.ppermute(value, 'seq', [(i, i ^ bit) for i in range(lax.axis_size('se...]
    dot_general x2 -> x1, matrix products: 18.6 us -> 13.6 us  [shards(): share = jnp.dot(attended, whole, preferred_element_type=jnp.float32)]
    unnamed x11 -> x7, local copies, waits for them, and re-layouts: 4.33 us -> 1.19 us
    pallas_call x2 -> x1, Pallas kernels: 36.2 us -> 34.9 us  [attention(): pl.pallas_call(functools.partial(attend, rows), out_shape=jax.ShapeDtypeS...]
  transfers between devices with their start and end apart: 10 -> 6, of which waited for: 7 -> 3; matrix products, arithmetic and copies ran while one was open for 6% -> 1% of each run, Pallas kernels for 16% -> 16%
where the time goes in v5:
time: 222 us; the launch traced here: 219 us
  waiting for transfers between devices  137 us (62%)
  Pallas kernels  34.9 us (16%)
  starting transfers between devices  14.8 us (7%)
  matrix products  13.6 us (6%)
  between operations  13.6 us (6%)
  other arithmetic  2.97 us (1%)
    all_gather x1, waiting for transfers between devices, shards(): whole = lax.all_gather(w_out, 'seq', axis=1, tiled=True)  83 us
    pallas_call x1, Pallas kernels, attention(): pl.pallas_call(functools.partial(attend, rows), out_shape=jax.ShapeDtypeS...  34.9 us
    ppermute x4, waiting for transfers between devices, from_behind(): lax.ppermute(value, 'seq', [(source, source + steps) for source in range(...  32.6 us
    ppermute x1, waiting for transfers between devices, exchange(): taken = lax.ppermute(give, 'head', [(0, 1), (1, 0)])  20.8 us
    dot_general x1, matrix products, shards(): share = jnp.dot(attended, whole, preferred_element_type=jnp.float32)  13.6 us
    ppermute x4, starting transfers between devices, from_behind(): lax.ppermute(value, 'seq', [(source, source + steps) for source in range(...  13.2 us
  transfers between devices with their start and end apart: 6, of which 3 were waited for; matrix products, arithmetic and copies ran while one was open for 1% of the time, Pallas kernels for 16%

profile of v5, /device:TPU:4, one launch (start us, length us, event | category | flops | bytes accessed | tf_op | source)
XLA Modules:
  0.0 218.5 jit_solution(9877104432320042110)
XLA Ops:
  6.5 0.0 copy-start.1
  6.5 0.0 copy-start.2
  6.5 0.0 all-gather.2.cloned.1.call-start
  6.5 0.7 all-gather.2.cloned.1.call-update
  7.3 0.2 copy-done.1
  7.5 0.2 copy.8
  7.7 0.0 copy-done.2
  7.7 0.1 fusion
  7.8 0.1 pad_maximum_fusion.1
  7.9 1.9 collective-permute-start.3
  9.8 3.4 %collective-permute-start.2 = (bf16[256,640]{1,0:T(8,128)(2,1)S(1)}, bf16[256,640]{1,0:T(8,128)(2,1)S(1)}, u32[]{:S(2)}, u32[]{:S(2)}) collective-permute-start(bf16[256,640]{1,0:T(8,128)(2,1)S(1)} %pad_maximum_fusion.1), channel_id=1, source_target_pairs={{0,4},{2,6},{4,8},{6,10},{8,12},{10,14},{12,16},{14,18},{16,20},{1... | collective-permute-start | bytes 983048 | tf_op jit(solution)/shard_map/ppermute | solution.py:23
  13.3 4.4 %collective-permute-start.1 = (bf16[256,640]{1,0:T(8,128)(2,1)S(1)}, bf16[256,640]{1,0:T(8,128)(2,1)S(1)}, u32[]{:S(2)}, u32[]{:S(2)}) collective-permute-start(bf16[256,640]{1,0:T(8,128)(2,1)S(1)} %pad_maximum_fusion.1), channel_id=1, source_target_pairs={{0,6},{2,8},{4,10},{6,12},{8,14},{10,16},{12,18},{14,20},{16,22},{... | collective-permute-start | bytes 983048 | tf_op jit(solution)/shard_map/ppermute | solution.py:23
  17.7 3.5 %collective-permute-start = (bf16[256,640]{1,0:T(8,128)(2,1)S(1)}, bf16[256,640]{1,0:T(8,128)(2,1)S(1)}, u32[]{:S(2)}, u32[]{:S(2)}) collective-permute-start(bf16[256,640]{1,0:T(8,128)(2,1)S(1)} %pad_maximum_fusion.1), channel_id=1, source_target_pairs={{0,8},{2,10},{4,12},{6,14},{8,16},{10,18},{12,20},{14,22},{16,24},... | collective-permute-start | bytes 983048 | tf_op jit(solution)/shard_map/ppermute | solution.py:23
  21.2 0.1 add_multiply_fusion
  21.3 0.1 pad_maximum_fusion.2.q_mark
  21.4 32.6 %collective-permute-done = bf16[256,640]{1,0:T(8,128)(2,1)S(1)} collective-permute-done((bf16[256,640]{1,0:T(8,128)(2,1)S(1)}, bf16[256,640]{1,0:T(8,128)(2,1)S(1)}, u32[]{:S(2)}, u32[]{:S(2)}) %collective-permute-start) | collective-permute-done | bytes 327712 | tf_op jit(solution)/shard_map/ppermute | solution.py:23
  54.0 0.1 slice_select_fusion.3
  54.1 0.1 maximum_dynamic-update-slice_fusion.3
  54.2 0.0 collective-permute-done.1
  54.2 0.1 slice_select_fusion.2
  54.3 0.1 maximum_dynamic-update-slice_fusion.2
  54.4 0.0 collective-permute-done.2
  54.4 0.1 slice_select_fusion.1
  54.5 0.1 maximum_dynamic-update-slice_fusion.1
  54.6 0.0 collective-permute-done.3
  54.7 0.1 slice_select_fusion
  54.7 0.1 maximum_dynamic-update-slice_fusion
  54.9 0.1 constant_dynamic-update-slice_fusion
  55.0 0.1 slice.61.content
  55.1 0.0 copy-start
  55.1 0.2 fusion.1
  55.3 0.2 slice_bitcast_fusion
  55.5 0.1 pad_maximum_fusion.tails
  55.6 0.7 copy-done
  56.3 34.9 %attention.1 = bf16[256,4096]{1,0:T(8,128)(2,1)S(1)} custom-call(bf16[256,4096]{1,0:T(8,128)(2,1)} %q_nope.1, bf16[256,2048]{1,0:T(8,128)(2,1)S(1)} %copy-done, bf16[256,128]{1,0:T(8,128)(2,1)S(1)} %pad_maximum_fusion.2.q_mark, bf16[1280,512]{1,0:T(8,128)(2,1)S(1)} %slice.61.content, bf16[2,1280,128]{2,1,0:T(8,128)(2,1)S(1)} %pad_maximum_fusion.tails, ...), custom_call_target="tpu_custom_call" | custom-call | flops 1048576 | bytes 1048576 | tf_op jit(solution)/shard_map/attention/pallas_call | solution.py:57
  91.2 83.0 %all-gather.2.cloned.1.call-done = bf16[4096,3584]{0,1:T(8,128)(2,1)} async-done(((bf16[4096,224]{0,1:T(8,128)(2,1)}), bf16[4096,3584]{0,1:T(8,128)(2,1)}) %all-gather.2.cloned.1.call-update) | async-done | bytes 29360144 | tf_op jit(solution)/shard_map/all_gather | solution.py:82
  174.2 13.6 %fusion.2 = f32[256,3584]{1,0:T(8,128)S(1)} fusion(bf16[256,4096]{1,0:T(8,128)(2,1)S(1)} %attention.1, bf16[4096,3584]{0,1:T(8,128)(2,1)} %all-gather.2.cloned.1.call-done), kind=kOutput, calls=%fused_computation.20 | convolution fusion | flops 7516192768 | bytes 35127296 | tf_op jit(solution)/shard_map/dot_general | solution.py:105
  187.8 0.2 select_convert_fusion
  188.0 1.6 collective-permute-start.4
  189.6 20.8 %collective-permute-done.4 = bf16[256,1792]{1,0:T(8,128)(2,1)S(1)} collective-permute-done((bf16[256,1792]{1,0:T(8,128)(2,1)S(1)}, bf16[256,1792]{1,0:T(8,128)(2,1)S(1)}, u32[]{:S(2)}, u32[]{:S(2)}) %collective-permute-start.4) | collective-permute-done | bytes 917536 | tf_op jit(solution)/shard_map/ppermute | solution.py:116
  210.4 1.3 add_convert_fusion
Async XLA Ops:
  6.5 1.0 copy-start.1
  6.5 1.2 copy-start.2
  6.5 167.7 %all-gather.2.cloned.1.call-start = ((), (), s32[]{:S(2)}) async-start(), calls=%async_computation | async-start | bytes 31195136 | tf_op jit(solution)/shard_map/all_gather | solution.py:82
  7.9 46.7 %collective-permute-start.3 = (bf16[256,640]{1,0:T(8,128)(2,1)S(1)}, bf16[256,640]{1,0:T(8,128)(2,1)S(1)}, u32[]{:S(2)}, u32[]{:S(2)}) collective-permute-start(bf16[256,640]{1,0:T(8,128)(2,1)S(1)} %pad_maximum_fusion.1), channel_id=1, source_target_pairs={{0,2},{2,4},{4,6},{6,8},{8,10},{10,12},{12,14},{14,16},{16,18},{18... | collective-permute-start | bytes 983048 | tf_op jit(solution)/shard_map/ppermute | solution.py:23
  9.8 44.6 %collective-permute-start.2 = (bf16[256,640]{1,0:T(8,128)(2,1)S(1)}, bf16[256,640]{1,0:T(8,128)(2,1)S(1)}, u32[]{:S(2)}, u32[]{:S(2)}) collective-permute-start(bf16[256,640]{1,0:T(8,128)(2,1)S(1)} %pad_maximum_fusion.1), channel_id=1, source_target_pairs={{0,4},{2,6},{4,8},{6,10},{8,12},{10,14},{12,16},{14,18},{16,20},{1... | collective-permute-start | bytes 983048 | tf_op jit(solution)/shard_map/ppermute | solution.py:23
  13.3 40.9 %collective-permute-start.1 = (bf16[256,640]{1,0:T(8,128)(2,1)S(1)}, bf16[256,640]{1,0:T(8,128)(2,1)S(1)}, u32[]{:S(2)}, u32[]{:S(2)}) collective-permute-start(bf16[256,640]{1,0:T(8,128)(2,1)S(1)} %pad_maximum_fusion.1), channel_id=1, source_target_pairs={{0,6},{2,8},{4,10},{6,12},{8,14},{10,16},{12,18},{14,20},{16,22},{... | collective-permute-start | bytes 983048 | tf_op jit(solution)/shard_map/ppermute | solution.py:23
  17.7 36.3 %collective-permute-start = (bf16[256,640]{1,0:T(8,128)(2,1)S(1)}, bf16[256,640]{1,0:T(8,128)(2,1)S(1)}, u32[]{:S(2)}, u32[]{:S(2)}) collective-permute-start(bf16[256,640]{1,0:T(8,128)(2,1)S(1)} %pad_maximum_fusion.1), channel_id=1, source_target_pairs={{0,8},{2,10},{4,12},{6,14},{8,16},{10,18},{12,20},{14,22},{16,24},... | collective-permute-start | bytes 983048 | tf_op jit(solution)/shard_map/ppermute | solution.py:23
  55.1 1.2 copy-start
  188.0 22.4 %collective-permute-start.4 = (bf16[256,1792]{1,0:T(8,128)(2,1)S(1)}, bf16[256,1792]{1,0:T(8,128)(2,1)S(1)}, u32[]{:S(2)}, u32[]{:S(2)}) collective-permute-start(bf16[256,1792]{1,0:T(8,128)(2,1)S(1)} %select_convert_fusion), channel_id=1, source_target_pairs={{0,1},{1,0},{2,3},{3,2},{4,5},{5,4},{6,7},{7,6},{8,9},{9,8},{10,11... | collective-permute-start | bytes 2752520 | tf_op jit(solution)/shard_map/ppermute | solution.py:116
Sparse Core Ops, SparseCore 0:
  9.0 165.2 all-gather.1
